TPU v7x, 128 devices: a whole 4x4x4 slice. The times are simulated.
128 devices in a mesh: comp: 2 (over core), tile: 64 (over z, y, x).
Axes of the slice: x: 4, y: 4, z: 4, core: 2. Of those that a mesh axis runs over, the one named last changes fastest.
Arguments:
- state: float32 [2, 8, 1024, 1024], P('comp', None, 'tile'), may hold values from -80 to 80, as said below
- basis: bfloat16 [12, 2, 8, 1024, 1024], P(None, 'comp', None, 'tile'), may hold values from -4 to 4
- kappa: float32 [2, 1024, 1024], P('comp', 'tile'), may hold values from 0.05 to 0.22
- vmix: float32 [2, 8, 8], P('comp'), may hold values from -1 to 1
- land_mask: int32 [1024, 1024], P('tile'), may hold values 0 or 1
- send_rows: int32 [2, 64, 64, 8], P('comp', 'tile'), may hold values from 0 to 127
- recv_slots: int32 [2, 64, 128, 4], P('comp', 'tile'), may hold values from 0 to 511
- recv_weights: float32 [2, 64, 128, 4], P('comp', 'tile'), may hold values from 0.1 to 0.4
Outputs:
- direction: float32 [2, 8, 1024, 1024], P('comp', None, 'tile')
- coefs: float32 [12], replicated
Inputs may be any that keep to these rules, and one draw needn't show every extreme that they name: `state`: the perturbation is noise plus a combination of the basis vectors.
All inputs are finite; a program needn't handle non-finite values. No bound on the sum of `land_mask` on one device may be relied on, other than what follows from the above.
Results may differ from a plain program's by a relative error of at most 0.0003.
Values sent between devices are 32-bit elements; how exact they have to be, the bound alone decides.
A program may use at most 64 MiB of HBM per device.

v0:
```python
import jax
import jax.numpy as jnp
from jax import lax
from jax.sharding import PartitionSpec as P

FLUX = 4
VECS = 12


def extended(cells, sides, width):
    for axis, dim in sides:
        count = lax.axis_size(axis)
        ends = count - 1
        head = lax.slice_in_dim(cells, 0, width, axis=dim)
        tail = lax.slice_in_dim(cells, cells.shape[dim] - width, cells.shape[dim], axis=dim)
        cells = jnp.concatenate(
            [
                lax.ppermute(tail, axis, [(i, (i + 1) % count) for i in range(ends)]),
                cells,
                lax.ppermute(head, axis, [((i + 1) % count, i) for i in range(ends)]),
            ],
            axis=dim,
        )
    return cells


def from_partner(block, axis, stride):
    count = lax.axis_size(axis)
    route = []
    for low in range(count):
        high = low | 1 << stride
        if high != low and high < count:
            route += [(low, high), (high, low)]
    return lax.ppermute(block, axis, route)


def advance(x, kap, vert_mat, maskf, forced):
    padded = extended(x, (("tile", 1),), 1)
    lap = padded[:, 2:] + padded[:, :-2] + jnp.roll(x, 1, -1) + jnp.roll(x, -1, -1) - 4.0 * x
    vert = jnp.einsum("lm,mrq->lrq", vert_mat, x, precision=lax.Precision.HIGHEST)
    return maskf * (x + kap * lap + vert + forced)


def body(state, basis, kappa, vmix, land_mask, send_rows, recv_slots, recv_weights):
    comp_id = lax.axis_index("comp")
    x = state[0]
    levels, rows, cols = x.shape
    nblk = rows * cols // 128
    surface = x[:FLUX].reshape(FLUX, nblk, 128)
    bucket = surface[:, send_rows[0, 0]]
    moved = lax.all_to_all(bucket, "tile", split_axis=1, concat_axis=1, tiled=True)
    arrived = from_partner(moved, "comp", 0)
    flat = arrived.reshape(FLUX, -1, 128)
    picked = flat[:, recv_slots[0, 0]]
    imported = jnp.einsum(
        "ek,fekq->feq", recv_weights[0, 0], picked, precision=lax.Precision.HIGHEST
    )
    imported = imported.reshape(FLUX, rows, cols)
    forced = jnp.concatenate([imported, jnp.zeros((levels - FLUX, rows, cols), jnp.float32)], 0)
    maskf = jnp.where(comp_id == 0, land_mask.astype(jnp.float32), jnp.float32(1.0))
    for step in range(2):
        x = advance(x, kappa[0], vmix[0], maskf, forced)
    total = float(levels * rows * cols * lax.axis_size("comp") * lax.axis_size("tile"))
    vflat = x.reshape(-1)
    qmat = basis[:, 0].reshape(VECS, -1)
    local_dots = jnp.dot(
        qmat, vflat, precision=lax.Precision.HIGHEST, preferred_element_type=jnp.float32
    )
    dots = lax.psum(local_dots, ("comp", "tile"))
    coefs = dots / total
    remain = vflat - jnp.dot(
        coefs, qmat, precision=lax.Precision.HIGHEST, preferred_element_type=jnp.float32
    )
    normsq = lax.psum(jnp.sum(remain * remain), ("comp", "tile"))
    direction = remain / jnp.sqrt(normsq / total + 1e-06)
    return (direction.reshape(1, levels, rows, cols), coefs)


def solution(mesh):
    return jax.shard_map(
        body,
        mesh=mesh,
        in_specs=(
            P("comp", None, "tile", None),
            P(None, "comp", None, "tile", None),
            P("comp", "tile", None),
            P("comp", None, None),
            P("tile", None),
            P("comp", "tile", None, None),
            P("comp", "tile", None, None),
            P("comp", "tile", None, None),
        ),
        out_specs=(P("comp", None, "tile", None), P()),
        check_vma=False,
    )
```

profile of v0, /device:TPU:1, one launch (start us, length us, event | category | flops | bytes accessed | tf_op | source)
XLA Modules:
  0.0 204.8 jit_solution(5193275752972541004)
XLA Ops:
  0.7 0.7 compare_select_fusion
  1.6 1.0 slice.68
  2.6 0.2 copy.17
  2.8 2.6 %gather_fusion = f32[512,4,128]{2,1,0:T(4,128)} fusion(f32[4,128,128]{2,0,1:T(4,128)S(1)} %copy.17, s32[1024]{0:T(1024)S(1)} %pad_clamp_fusion.1), kind=kCustom, calls=%fused_computation | custom fusion | bytes 2099200 | tf_op jit(solution)/shard_map/gather | solution.py:50
  5.5 12.0 %all-to-all-start = ((f32[4,64,8,128]{3,0,2,1:T(4,128)}), f32[4,64,8,128]{3,0,2,1:T(4,128)S(1)}, u32[]{:S(2)}, u32[]{:S(2)}) async-start(f32[4,64,8,128]{3,0,2,1:T(4,128)} %bitcast.6), calls=%async_computation | async-start | bytes 2097152 | tf_op jit(solution)/shard_map/all_to_all | solution.py:51
  17.4 0.3 copy.28
  17.8 1.3 collective-permute-start
  19.1 4.6 %collective-permute-start.1 = (f32[8,1,1024]{2,0,1:T(8,128)S(1)}, f32[8,1,1024]{2,0,1:T(8,128)}, u32[]{:S(2)}, u32[]{:S(2)}) collective-permute-start(f32[8,1,1024]{2,0,1:T(8,128)S(1)} %get-tuple-element.15), channel_id=1, source_target_pairs={{0,1},{1,2},{2,3},{3,4},{4,5},{5,6},{6,7},{7,8},{8,9},{9,10},{10,1... | collective-permute-start | bytes 98312 | tf_op jit(solution)/shard_map/ppermute | solution.py:18
  23.7 11.4 %all-to-all-done = f32[4,64,8,128]{3,0,2,1:T(4,128)S(1)} async-done(((f32[4,64,8,128]{3,0,2,1:T(4,128)}), f32[4,64,8,128]{3,0,2,1:T(4,128)S(1)}, u32[]{:S(2)}, u32[]{:S(2)}) %all-to-all-start) | async-done | bytes 1048608 | tf_op jit(solution)/shard_map/all_to_all | solution.py:51
  35.0 2.6 %collective-permute-start.2 = (f32[4,64,8,128]{3,0,2,1:T(4,128)S(1)}, f32[4,64,8,128]{3,0,2,1:T(4,128)S(1)}, u32[]{:S(2)}, u32[]{:S(2)}) collective-permute-start(f32[4,64,8,128]{3,0,2,1:T(4,128)S(1)} %all-to-all-done), channel_id=1, source_target_pairs={{0,64},{64,0},{1,65},{65,1},{2,66},{66,2},{3,67},{67,3},{4,68},{68... | collective-permute-start | bytes 3145736 | tf_op jit(solution)/shard_map/ppermute | solution.py:34
  37.6 0.1 copy.18
  37.9 0.1 copy.21
  38.0 2.3 %pad.27 = bf16[16,128,1024]{2,1,0:T(8,128)(2,1)S(1)} pad(bf16[12,128,1024]{2,1,0:T(8,128)(2,1)} %bitcast.71, bf16[]{:T(256)} %constant.52), padding=0_4x0_0x0_0 | pad | bytes 7340034
  40.3 4.3 %copy.24 = bf16[2,8,128,1024]{3,1,2,0:T(8,128)(2,1)} copy(bf16[2,8,128,1024]{3,2,1,0:T(8,128)(2,1)S(1)} %bitcast.64) | data formatting | bytes 8388608
  44.7 0.9 fusion.26
  45.7 2.1 %gather_fusion.1 = f32[512,4,128]{2,1,0:T(4,128)S(1)} fusion(f32[4,512,128]{2,0,1:T(4,128)S(1)} %bitcast.74, s32[1024]{0:T(1024)S(1)} %pad_clamp_fusion), kind=kCustom, calls=%fused_computation.1 | custom fusion | bytes 2099200 | tf_op jit(solution)/shard_map/gather | solution.py:54
  47.7 2.0 fusion.5
  49.8 2.0 fusion.4
  51.8 0.2 fusion.23
  52.0 1.3 collective-permute-start.3
  53.3 4.2 %collective-permute-start.4 = (f32[8,1,1024]{2,0,1:T(8,128)S(1)}, f32[8,1,1024]{2,0,1:T(8,128)S(1)}, u32[]{:S(2)}, u32[]{:S(2)}) collective-permute-start(f32[8,1,1024]{2,0,1:T(8,128)S(1)} %get-tuple-element.9), channel_id=1, source_target_pairs={{0,1},{1,2},{2,3},{3,4},{4,5},{5,6},{6,7},{7,8},{8,9},{9,10},{10,1... | collective-permute-start | bytes 98312 | tf_op jit(solution)/shard_map/ppermute | solution.py:18
  57.6 0.7 collective-permute-done.4
  58.3 0.9 fusion.2
  59.2 0.3 copy.19
  59.5 0.6 reshape.104
  60.1 6.5 %convolution_bitcast_fusion.1 = f32[12]{0:T(128)S(1)} fusion(f32[131072,1]{0,1:T(1,128)S(1)} %reshape.104, bf16[12,131072]{1,0:T(8,128)(2,1)} %bitcast.62), kind=kOutput, calls=%fused_computation.9 | convolution fusion | flops 18874368 | bytes 3670064 | tf_op jit(solution)/shard_map/dot_general | solution.py:66
  66.6 0.1 copy.23
  66.7 68.6 %psum.14 = f32[12]{0:T(128)S(1)} all-reduce(f32[12]{0:T(128)S(1)} %convolution_bitcast_fusion.1), channel_id=1, replica_groups=mesh['comp'=2,'tile'=64] {'comp','tile'}, use_global_device_ids=true, to_apply=%region_0.1 | all-reduce | flops 12 | bytes 96 | tf_op jit(solution)/shard_map/psum | solution.py:69
  135.3 4.0 %fusion.21 = f32[1,131072]{1,0:T(1,128)S(1)} fusion(bf16[12,131072]{1,0:T(8,128)(2,1)} %bitcast.63, f32[12]{0:T(128)S(1)} %broadcast_multiply_fusion), kind=kOutput, calls=%fused_computation.38 | convolution fusion | flops 18874368 | bytes 3670064 | tf_op jit(solution)/shard_map/dot_general | solution.py:71
  139.3 0.8 multiply_reduce_fusion
  140.1 63.1 %psum.15 = f32[]{:T(128)} all-reduce(f32[]{:T(128)} %get-tuple-element.2), channel_id=1, replica_groups=mesh['comp'=2,'tile'=64] {'comp','tile'}, use_global_device_ids=true, to_apply=%region_2.3 | all-reduce | flops 1 | bytes 8 | tf_op jit(solution)/shard_map/psum | solution.py:74
  203.9 0.9 reshape.82
  (32 shorter events, 0.6 us)
Async XLA Ops:
  0.6 49.2 %copy-start = (f32[1,8,8]{2,1,0:T(8,128)S(1)}, f32[1,8,8]{2,1,0:T(8,128)}, u32[]{:S(2)}) copy-start(f32[1,8,8]{2,1,0:T(8,128)} %param.11) | copy-start | bytes 772
  0.6 16.8 %copy-start.1 = (f32[1,8,16,1024]{3,2,1,0:T(8,128)S(1)}, f32[1,8,16,1024]{3,2,1,0:T(8,128)}, u32[]{:S(2)}) copy-start(f32[1,8,16,1024]{3,2,1,0:T(8,128)} %param.8) | copy-start | bytes 1572868
  0.7 37.0 %copy-start.4 = (s32[1,1,128,4]{2,3,1,0:T(4,128)S(1)}, s32[1,1,128,4]{2,3,1,0:T(4,128)}, u32[]{:S(2)}) copy-start(s32[1,1,128,4]{2,3,1,0:T(4,128)} %param.14) | copy-start | bytes 6148
  0.7 37.2 %copy-start.3 = (f32[1,1,128,4]{2,3,1,0:T(4,128)S(1)}, f32[1,1,128,4]{2,3,1,0:T(4,128)}, u32[]{:S(2)}) copy-start(f32[1,1,128,4]{2,3,1,0:T(4,128)} %param.15) | copy-start | bytes 6148
  5.5 29.6 %all-to-all-start = ((f32[4,64,8,128]{3,0,2,1:T(4,128)}), f32[4,64,8,128]{3,0,2,1:T(4,128)S(1)}, u32[]{:S(2)}, u32[]{:S(2)}) async-start(f32[4,64,8,128]{3,0,2,1:T(4,128)} %bitcast.6), calls=%async_computation | async-start | bytes 2097152 | tf_op jit(solution)/shard_map/all_to_all | solution.py:51
  17.8 32.0 %collective-permute-start = (f32[8,1,1024]{2,0,1:T(8,128)S(1)}, f32[8,1,1024]{2,0,1:T(8,128)}, u32[]{:S(2)}, u32[]{:S(2)}) collective-permute-start(f32[8,1,1024]{2,0,1:T(8,128)S(1)} %get-tuple-element.14), channel_id=1, source_target_pairs={{1,0},{2,1},{3,2},{4,3},{5,4},{6,5},{7,6},{8,7},{9,8},{10,9},{11,1... | collective-permute-start | bytes 98312 | tf_op jit(solution)/shard_map/ppermute | solution.py:20
  19.1 30.7 %collective-permute-start.1 = (f32[8,1,1024]{2,0,1:T(8,128)S(1)}, f32[8,1,1024]{2,0,1:T(8,128)}, u32[]{:S(2)}, u32[]{:S(2)}) collective-permute-start(f32[8,1,1024]{2,0,1:T(8,128)S(1)} %get-tuple-element.15), channel_id=1, source_target_pairs={{0,1},{1,2},{2,3},{3,4},{4,5},{5,6},{6,7},{7,8},{8,9},{9,10},{10,1... | collective-permute-start | bytes 98312 | tf_op jit(solution)/shard_map/ppermute | solution.py:18
  35.0 10.6 %collective-permute-start.2 = (f32[4,64,8,128]{3,0,2,1:T(4,128)S(1)}, f32[4,64,8,128]{3,0,2,1:T(4,128)S(1)}, u32[]{:S(2)}, u32[]{:S(2)}) collective-permute-start(f32[4,64,8,128]{3,0,2,1:T(4,128)S(1)} %all-to-all-done), channel_id=1, source_target_pairs={{0,64},{64,0},{1,65},{65,1},{2,66},{66,2},{3,67},{67,3},{4,68},{68... | collective-permute-start | bytes 3145736 | tf_op jit(solution)/shard_map/ppermute | solution.py:34
  40.3 4.3 %copy-start.2 = (s32[16,1024]{1,0:T(8,128)S(1)}, s32[16,1024]{1,0:T(8,128)}, u32[]{:S(2)}) copy-start(s32[16,1024]{1,0:T(8,128)} %param.12) | copy-start | bytes 196612
  44.6 5.2 %copy-start.6 = (f32[1,16,1024]{2,1,0:T(8,128)S(1)}, f32[1,16,1024]{2,1,0:T(8,128)}, u32[]{:S(2)}) copy-start(f32[1,16,1024]{2,1,0:T(8,128)} %param.10) | copy-start | bytes 196612
  52.0 5.6 %collective-permute-start.3 = (f32[8,1,1024]{2,0,1:T(8,128)S(1)}, f32[8,1,1024]{2,0,1:T(8,128)S(1)}, u32[]{:S(2)}, u32[]{:S(2)}) collective-permute-start(f32[8,1,1024]{2,0,1:T(8,128)S(1)} %get-tuple-element.8), channel_id=1, source_target_pairs={{1,0},{2,1},{3,2},{4,3},{5,4},{6,5},{7,6},{8,7},{9,8},{10,9},{11,1... | collective-permute-start | bytes 98312 | tf_op jit(solution)/shard_map/ppermute | solution.py:20
  53.3 5.0 %collective-permute-start.4 = (f32[8,1,1024]{2,0,1:T(8,128)S(1)}, f32[8,1,1024]{2,0,1:T(8,128)S(1)}, u32[]{:S(2)}, u32[]{:S(2)}) collective-permute-start(f32[8,1,1024]{2,0,1:T(8,128)S(1)} %get-tuple-element.9), channel_id=1, source_target_pairs={{0,1},{1,2},{2,3},{3,4},{4,5},{5,6},{6,7},{7,8},{8,9},{9,10},{10,1... | collective-permute-start | bytes 98312 | tf_op jit(solution)/shard_map/ppermute | solution.py:18
  135.3 68.6 %copy-start.5 = (f32[12]{0:T(128)}, f32[12]{0:T(128)S(1)}, u32[]{:S(2)}) copy-start(f32[12]{0:T(128)S(1)} %broadcast_multiply_fusion) | copy-start | bytes 148
where the time goes:
time: 205 us
  blocking collectives  132 us (64%)
  starting transfers between devices  25.9 us (13%)
  local copies, waits for them, and re-layouts  16.6 us (8%)
  matrix products  15.3 us (7%)
  waiting for transfers between devices  12.1 us (6%)
    psum x1, blocking collectives, body(): dots = lax.psum(local_dots, ('comp', 'tile'))  68.6 us
    psum x1, blocking collectives, body(): normsq = lax.psum(jnp.sum(remain * remain), ('comp', 'tile'))  63.1 us
    all_to_all x1, starting transfers between devices, body(): lax.all_to_all(bucket, 'tile', split_axis=1, concat_axis=1, tiled=True)  12 us
    all_to_all x1, waiting for transfers between devices, body(): lax.all_to_all(bucket, 'tile', split_axis=1, concat_axis=1, tiled=True)  11.4 us
    ppermute x2, starting transfers between devices, extended(): lax.ppermute(tail, axis, [(i, (i + 1) % count) for i in range(ends)])  8.77 us
    unnamed x18, local copies, waits for them, and re-layouts  7.05 us
    dot_general x1, matrix products, body(): jnp.dot(qmat, vflat, precision=lax.Precision.HIGHEST, preferred_element_t...  6.49 us
  transfers between devices with their start and end apart: 6, of which 2 were waited for; matrix products, arithmetic and copies ran while one was open for 6% of the time, Pallas kernels for 0%

commit v1 on v0

v1 whole, which is shorter than its diff:
```python
import functools

import jax
import jax.numpy as jnp
from jax import lax
from jax.experimental import pallas as pl
from jax.experimental.pallas import tpu as pltpu
from jax.sharding import PartitionSpec as P

FLUX = 4
VECS = 12
LEV = 8
ROWS = 16
COLS = 1024
TILES = 64
CAP = 8
NB = 128
GROUPS = 4
PER = TILES // GROUPS
MESH = pl.DeviceIdType.MESH
F32 = jnp.float32
BF16 = jnp.bfloat16
PAIRS = [(i, j) for i in range(VECS) for j in range(i, VECS)]


def hops(k):
    return sum((0, 1, 2, 1)[(k >> s) & 3] for s in (0, 2, 4))


PEERS = [sorted((k for k in range(1, TILES) if k & 1 == c), key=lambda k: -hops(k)) for c in (0, 1)]


def offset_of(step):
    a, b, c = step & 3, (step >> 2) & 3, step >> 4
    return a, (a + b) & 3, (a + c) & 3


def moved_tile(tile, step):
    dx, dy, dz = offset_of(step)
    return ((tile & 3) + dx & 3) | (((tile >> 2 & 3) + dy & 3) << 2) | (((tile >> 4) + dz & 3) << 4)


def remote(src, dst, send, recv, comp, tile):
    return pltpu.make_async_remote_copy(
        src_ref=src, dst_ref=dst, send_sem=send, recv_sem=recv, device_id=(comp, tile), device_id_type=MESH
    )


def wait_bytes(ref, sem):
    pltpu.make_async_copy(ref, ref, sem).wait()


def sum_over_devices(comp, tile, mine, pair, wide, part, other, sems):
    first = remote(mine, pair, sems.at[0], sems.at[1], 1 - comp, tile)
    first.start()
    first.wait()
    chip = mine[...] + pair[...]
    part[...] = chip
    odd = tile & 1
    slot = tile >> 1

    for c in (0, 1):

        @pl.when(comp == c)
        def _():
            for k in PEERS[c]:
                remote(part, wide.at[slot], sems.at[2], sems.at[3], odd, tile ^ k).start()

    @pl.when(comp == odd)
    def _():
        wide[slot] = chip
        wait_bytes(wide.at[pl.ds(0, TILES // 2 - 1)], sems.at[3])

    @pl.when(comp != odd)
    def _():
        wait_bytes(wide.at[pl.ds(0, TILES // 2)], sems.at[3])

    half = wide[0]
    for s in range(1, TILES // 2):
        half = half + wide[s]
    for c in (0, 1):

        @pl.when(comp == c)
        def _():
            wait_bytes(wide.at[pl.ds(0, len(PEERS[c]))], sems.at[2])

    part[...] = half
    last = remote(part, other, sems.at[4], sems.at[5], 1 - comp, tile)
    last.start()
    last.wait()
    return half + other[...]


def stencil(ref, level, kap):
    x = ref[level, 8:24, :]
    lap = (
        ref[level, 7:23, :]
        + ref[level, 9:25, :]
        + pltpu.roll(x, 1, 1)
        + pltpu.roll(x, COLS - 1, 1)
        - 4.0 * x
    )
    return x + kap * lap


def mixed(ref, vmix, level, count):
    total = vmix[0, level, 0] * ref[0, 8:24, :]
    for m in range(1, count):
        total = total + vmix[0, level, m] * ref[m, 8:24, :]
    return total


def kernel(
    state, basis, kappa, land, slots, weights, vmix, rows, direction, coefs,
    x0, x1, y, fh, f, basis_v, kap, land_v, maskf, surf, bucket, arrived, imp,
    g_mine, g_pair, g_wide, g_part, g_other, e_mine, e_pair, e_wide, e_part, e_other,
    load, send, recv, halo, gsem, esem, store,
):
    comp = lax.axis_index("comp")
    tile = lax.axis_index("tile")
    total = float(LEV * ROWS * COLS * TILES * 2)
    above = tile - 1 & TILES - 1
    below = tile + 1 & TILES - 1

    surf_loads = [
        pltpu.make_async_copy(
            state.at[0, pl.ds(0, FLUX), :, pl.ds(128 * j, 128)], surf.at[j], load.at[0]
        )
        for j in range(8)
    ]
    for c in surf_loads:
        c.start()
    x_load = pltpu.make_async_copy(state.at[0], x0.at[:, pl.ds(8, ROWS), :], load.at[1])
    x_load.start()
    barrier = pltpu.get_barrier_semaphore()

    def greet(step, carry):
        pl.semaphore_signal(barrier, inc=1, device_id=(1 - comp, moved_tile(tile, step)), device_id_type=MESH)
        return carry

    lax.fori_loop(0, TILES, greet, 0)
    for t in (above, below):
        pl.semaphore_signal(barrier, inc=1, device_id=(comp, t), device_id_type=MESH)
    kap_load = pltpu.make_async_copy(kappa.at[0], kap, load.at[2])
    kap_load.start()
    land_load = pltpu.make_async_copy(land, land_v, load.at[3])
    land_load.start()
    basis_load = pltpu.make_async_copy(basis.at[:, 0], basis_v, load.at[4])
    basis_load.start()
    for c in surf_loads:
        c.wait()
    x_load.wait()
    pl.semaphore_wait(barrier, TILES + 2)

    def swap_rows(ref, sems):
        up = remote(ref.at[:, pl.ds(8, 1), :], ref.at[:, pl.ds(24, 1), :], sems.at[0], sems.at[1], comp, above)
        down = remote(ref.at[:, pl.ds(23, 1), :], ref.at[:, pl.ds(7, 1), :], sems.at[2], sems.at[3], comp, below)
        up.start()
        down.start()
        return up, down

    def clear_ends(ref):
        n = ref.shape[0]

        @pl.when(tile == 0)
        def _():
            ref[:, 7:8, :] = jnp.zeros((n, 1, COLS), F32)

        @pl.when(tile == TILES - 1)
        def _():
            ref[:, 24:25, :] = jnp.zeros((n, 1, COLS), F32)

    swap0 = swap_rows(x0, halo.at[0])

    flat_surf = surf.reshape(8 * FLUX * ROWS, 128)
    flat_bucket = bucket.reshape(TILES * FLUX * CAP, 128)

    def deliver(step, carry):
        dest = moved_tile(tile, step)
        for j in range(CAP):
            blk = rows[0, 0, dest, j]
            start = (blk & 7) * (FLUX * ROWS) + (blk >> 3)
            flat_bucket[pl.ds(step * (FLUX * CAP) + j, FLUX, stride=CAP), :] = flat_surf[
                pl.ds(start, FLUX, stride=ROWS), :
            ]
        remote(bucket.at[step], arrived.at[step], send, recv.at[step >> 4], 1 - comp, dest).start()
        return carry

    lax.fori_loop(0, TILES, deliver, 0)

    basis_load.wait()
    lane = lax.broadcasted_iota(jnp.int32, (16, 128), 1)
    sub = lax.broadcasted_iota(jnp.int32, (16, 128), 0)
    rows_of = {}
    third = len(PAIRS) // 3
    for part in range(3):
        pairs = PAIRS[part * third : (part + 1) * third]

        def gram_step(n, acc, pairs=pairs):
            level = n >> 3
            at = pl.multiple_of((n & 7) * 128, 128)
            used = sorted({i for p in pairs for i in p})
            vals = {i: basis_v[i, level, :, pl.ds(at, 128)].astype(F32) for i in used}
            out = []
            for (i, j), a in zip(pairs, acc):
                p = vals[i] * vals[j]
                out.append(a + (p[:8] + p[8:]))
            return tuple(out)

        acc = lax.fori_loop(0, 64, gram_step, tuple(jnp.zeros((8, 128), F32) for _ in pairs))
        for p, a in zip(pairs, acc):
            rows_of[p] = jnp.sum(a, axis=0, keepdims=True)
    gram_here = jnp.zeros((16, 128), F32)
    for i in range(VECS):
        stack = jnp.concatenate(
            [rows_of[(min(i, j), max(i, j))] for j in range(VECS)] + [jnp.zeros((4, 128), F32)], axis=0
        )
        gram_here = jnp.where(lane == i, jnp.sum(stack, axis=1, keepdims=True), gram_here)
    g_mine[...] = gram_here

    kap_load.wait()
    land_load.wait()
    maskf[...] = jnp.where(comp == 0, land_v[...].astype(F32), jnp.ones((ROWS, COLS), F32))
    for c in swap0:
        c.wait()
    clear_ends(x0)
    for l in range(LEV):
        x1[l, 8:24, :] = maskf[...] * (stencil(x0, l, kap[...]) + mixed(x0, vmix, l, LEV))
    swap1 = swap_rows(x1, halo.at[1])
    gram = sum_over_devices(comp, tile, g_mine, g_pair, g_wide, g_part, g_other, gsem)
    for c in swap1:
        c.wait()
    clear_ends(x1)
    for l in range(LEV):
        y[l] = maskf[...] * (stencil(x1, l, kap[...]) + mixed(x1, vmix, l, LEV))

    slot = slots[0, 0]
    weight = weights[0, 0]
    src = slot >> 3
    a = (tile & 3) - (src & 3) & 3
    b = (tile >> 2 & 3) - (src >> 2 & 3) - a & 3
    c = (tile >> 4) - (src >> 4) - a & 3
    place = (a | b << 2 | c << 4) * CAP + (slot & 7)
    at_lane = lax.broadcasted_iota(jnp.int32, (NB, TILES * CAP), 1)
    matrix = jnp.zeros((NB, TILES * CAP), F32)
    for k in range(4):
        matrix = matrix + jnp.where(at_lane == place[:, k : k + 1], weight[:, k : k + 1], 0.0)
    high = matrix.astype(BF16)
    low = (matrix - high.astype(F32)).astype(BF16)
    dot = functools.partial(jnp.dot, preferred_element_type=F32)
    sums = jnp.zeros((NB, FLUX * 128), F32)
    for g in range(GROUPS):
        wait_bytes(arrived.at[pl.ds(g * PER, PER)], recv.at[g])
        got = jnp.concatenate(
            [arrived[g * PER : (g + 1) * PER, i].reshape(PER * CAP, 128) for i in range(FLUX)], axis=1
        )
        got_high = got.astype(BF16)
        got_low = (got - got_high.astype(F32)).astype(BF16)
        cut = slice(g * PER * CAP, (g + 1) * PER * CAP)
        sums = sums + dot(high[:, cut], got_high) + dot(low[:, cut], got_high) + dot(high[:, cut], got_low)
    for i in range(FLUX):
        imp[i * NB : (i + 1) * NB, :] = sums[:, i * 128 : (i + 1) * 128]
    for i in range(FLUX):
        for j in range(8):
            piece = imp[pl.ds(i * NB + j, ROWS, stride=8), :]
            f[i, :, j * 128 : (j + 1) * 128] = piece
            fh[i, 8:24, j * 128 : (j + 1) * 128] = maskf[:, j * 128 : (j + 1) * 128] * piece
    swap2 = swap_rows(fh, halo.at[2])
    for c in swap2:
        c.wait()
    clear_ends(fh)
    for l in range(LEV):
        z = mixed(fh, vmix, l, FLUX)
        if l < FLUX:
            z = z + stencil(fh, l, kap[...]) + f[l]
        y[l] = y[l] + maskf[...] * z

    def dot_step(n, acc):
        level = n >> 3
        at = pl.multiple_of((n & 7) * 128, 128)
        x = y[level, :, pl.ds(at, 128)]
        out = [a + basis_v[i, level, :, pl.ds(at, 128)].astype(F32) * x for i, a in enumerate(acc[:VECS])]
        return tuple(out) + (acc[VECS] + x * x,)

    acc = lax.fori_loop(0, 64, dot_step, tuple(jnp.zeros((16, 128), F32) for _ in range(VECS + 1)))
    stack = jnp.concatenate([jnp.sum(a, axis=0, keepdims=True) for a in acc] + [jnp.zeros((3, 128), F32)], axis=0)
    col = jnp.sum(stack, axis=1, keepdims=True)
    e_mine[...] = jnp.sum(jnp.where(lane == sub, col, 0.0), axis=0, keepdims=True)
    dots = sum_over_devices(comp, tile, e_mine, e_pair, e_wide, e_part, e_other, esem)
    first = lax.broadcasted_iota(jnp.int32, (1, 128), 1)
    coef = jnp.where(first < VECS, dots * (1.0 / total), 0.0)
    coefs[...] = coef
    coef_col = jnp.sum(jnp.where(lane == sub, jnp.broadcast_to(coef, (16, 128)), 0.0), axis=1, keepdims=True)
    square = jnp.sum(jnp.where(first == VECS, dots, 0.0) - 2.0 * dots * coef, axis=1, keepdims=True)
    gc = jnp.sum(gram * coef, axis=1, keepdims=True)
    square = square + jnp.sum(gc * coef_col, axis=0, keepdims=True)
    scale = 1.0 / jnp.sqrt(jnp.maximum(square, 0.0) * (1.0 / total) + 1e-06)
    weigh = [jnp.broadcast_to(coef_col[i : i + 1] * scale, (16, 128)) for i in range(VECS)]
    scale = jnp.broadcast_to(scale, (16, 128))

    for l in range(LEV):

        def finish(n, carry):
            at = pl.multiple_of(n * 128, 128)
            w = scale * y[l, :, pl.ds(at, 128)]
            for i in range(VECS):
                w = w - weigh[i] * basis_v[i, l, :, pl.ds(at, 128)].astype(F32)
            y[l, :, pl.ds(at, 128)] = w
            return carry

        lax.fori_loop(0, 8, finish, 0)
        pltpu.make_async_copy(y.at[l], direction.at[0, l], store).start()
    wait_bytes(bucket, send)
    wait_bytes(y, store)


def body(state, basis, kappa, vmix, land_mask, send_rows, recv_slots, recv_weights):
    anywhere = pl.BlockSpec(memory_space=pl.ANY)
    vmem = pl.BlockSpec(memory_space=pltpu.VMEM)
    smem = pl.BlockSpec(memory_space=pltpu.SMEM)
    dma = pltpu.SemaphoreType.DMA
    pad = (LEV, 32, COLS)
    direction, coefs = pl.pallas_call(
        kernel,
        out_shape=(
            jax.ShapeDtypeStruct((1, LEV, ROWS, COLS), F32),
            jax.ShapeDtypeStruct((1, 128), F32),
        ),
        in_specs=[anywhere, anywhere, anywhere, anywhere, vmem, vmem, smem, smem],
        out_specs=(anywhere, vmem),
        scratch_shapes=[
            pltpu.VMEM(pad, F32),
            pltpu.VMEM(pad, F32),
            pltpu.VMEM((LEV, ROWS, COLS), F32),
            pltpu.VMEM((FLUX, 32, COLS), F32),
            pltpu.VMEM((FLUX, ROWS, COLS), F32),
            pltpu.VMEM((VECS, LEV, ROWS, COLS), BF16),
            pltpu.VMEM((ROWS, COLS), F32),
            pltpu.VMEM((ROWS, COLS), jnp.int32),
            pltpu.VMEM((ROWS, COLS), F32),
            pltpu.VMEM((8, FLUX, ROWS, 128), F32),
            pltpu.VMEM((TILES, FLUX, CAP, 128), F32),
            pltpu.VMEM((TILES, FLUX, CAP, 128), F32),
            pltpu.VMEM((FLUX * NB, 128), F32),
            pltpu.VMEM((16, 128), F32),
            pltpu.VMEM((16, 128), F32),
            pltpu.VMEM((TILES // 2, 16, 128), F32),
            pltpu.VMEM((16, 128), F32),
            pltpu.VMEM((16, 128), F32),
            pltpu.VMEM((1, 128), F32),
            pltpu.VMEM((1, 128), F32),
            pltpu.VMEM((TILES // 2, 1, 128), F32),
            pltpu.VMEM((1, 128), F32),
            pltpu.VMEM((1, 128), F32),
            dma((5,)),
            dma(()),
            dma((GROUPS,)),
            dma((3, 4)),
            dma((6,)),
            dma((6,)),
            dma(()),
        ],
        compiler_params=pltpu.CompilerParams(
            collective_id=0, has_side_effects=True, vmem_limit_bytes=56 << 20
        ),
        name="interval",
    )(state, basis, kappa, land_mask, recv_slots, recv_weights, vmix, send_rows)
    return direction, coefs[0, :VECS]


def solution(mesh):
    return jax.shard_map(
        body,
        mesh=mesh,
        in_specs=(
            P("comp", None, "tile", None),
            P(None, "comp", None, "tile", None),
            P("comp", "tile", None),
            P("comp", None, None),
            P("tile", None),
            P("comp", "tile", None, None),
            P("comp", "tile", None, None),
            P("comp", "tile", None, None),
        ),
        out_specs=(P("comp", None, "tile", None), P()),
        check_vma=False,
    )
```

time: 205 us -> 58.7 us (0.29)
  blocking collectives: 132 us -> 0 us
  Pallas kernels: 0 us -> 50.5 us
  starting transfers between devices: 25.9 us -> 0 us
  matrix products: 15.3 us -> 0 us
  waiting for transfers between devices: 12.1 us -> 0 us
  local copies, waits for them, and re-layouts: 16.6 us -> 7.22 us
    psum x2 -> x0, blocking collectives: 132 us -> none  [the longest x1 68.6 us: body(): dots = lax.psum(local_dots, ('comp', 'tile'))]
    pallas_call x0 -> x1, Pallas kernels: none -> 50.5 us  [body(): pl.pallas_call(kernel, out_shape=(jax.ShapeDtypeStruct((1, LEV, ROWS, COL...]
    dot_general x5 -> x0, matrix products: 15.3 us -> none  [the longest x1 6.49 us: body(): jnp.dot(qmat, vflat, precision=lax.Precision.HIGHEST, preferred_element_t...]
    ppermute x5 -> x0, starting transfers between devices: 13.9 us -> none  [the longest x2 8.77 us: extended(): lax.ppermute(tail, axis, [(i, (i + 1) % count) for i in range(ends)])]
    all_to_all x1 -> x0, starting transfers between devices: 12 us -> none  [body(): lax.all_to_all(bucket, 'tile', split_axis=1, concat_axis=1, tiled=True)]
    all_to_all x1 -> x0, waiting for transfers between devices: 11.4 us -> none  [body(): lax.all_to_all(bucket, 'tile', split_axis=1, concat_axis=1, tiled=True)]
    gather x2 -> x0, local copies, waits for them, and re-layouts: 4.71 us -> none  [the longest x1 2.63 us: body(): bucket = surface[:, send_rows[0, 0]]]
    slice x7 -> x0, local copies, waits for them, and re-layouts: 2.3 us -> none  [the longest x4 1.31 us: advance(): jnp.roll(x, -1, -1)]
  transfers between devices with their start and end apart: 6 -> 0, of which waited for: 2 -> 0; matrix products, arithmetic and copies ran while one was open for 6% -> 0% of each run, Pallas kernels for 0% -> 0%
where the time goes in v1:
time: 58.7 us; the launch traced here: 58.4 us
  Pallas kernels  50.5 us (86%)
  local copies, waits for them, and re-layouts  7.22 us (12%)
  between operations  0.64 us (1%)
    pallas_call x1, Pallas kernels, body(): pl.pallas_call(kernel, out_shape=(jax.ShapeDtypeStruct((1, LEV, ROWS, COL...  50.5 us
    unnamed x4, local copies, waits for them, and re-layouts  6.11 us

profile of v1, /device:TPU:1, one launch (start us, length us, event | category | flops | bytes accessed | tf_op | source)
XLA Modules:
  0.0 58.4 jit_solution(7527195209415533146)
XLA Ops:
  0.6 1.4 %copy.12.rows = s32[1,1,64,8]{3,2,1,0:T(8,128)} copy(s32[1,1,64,8]{2,3,1,0:T(8,128)} %param.13) | data formatting | bytes 4096 | tf_op args[5]
  2.0 1.4 %copy.10.slots = s32[1,1,128,4]{3,2,1,0:T(8,128)} copy(s32[1,1,128,4]{2,3,1,0:T(4,128)} %param.14) | data formatting | bytes 4096 | tf_op args[6]
  3.4 1.4 %copy.11.weights = f32[1,1,128,4]{3,2,1,0:T(8,128)} copy(f32[1,1,128,4]{2,3,1,0:T(4,128)} %param.15) | data formatting | bytes 4096 | tf_op args[7]
  4.9 50.5 %interval.1 = (f32[1,8,16,1024]{3,2,1,0:T(8,128)}, f32[1,128]{1,0:T(1,128)}) custom-call(f32[1,8,16,1024]{3,2,1,0:T(8,128)} %state.1, bf16[12,1,8,16,1024]{4,3,2,1,0:T(8,128)(2,1)} %basis.1, f32[1,16,1024]{2,1,0:T(8,128)} %kappa.1, s32[16,1024]{1,0:T(8,128)} %land.1, s32[1,1,128,4]{3,2,1,0:T(8,128)} %copy.10.slots, f32[1,1,128,4]{3,2,1,0:T(8,128)} %copy.11.weights, ...), custom_call_target="tpu_custom_call" | custom-call | tf_op jit(solution)/shard_map/interval/pallas_call | solution.py:323
  55.4 1.1 %slice_bitcast_fusion = f32[12]{0:T(128)} fusion(f32[1,128]{1,0:T(1,128)} %get-tuple-element.5), kind=kLoop, calls=%fused_computation | loop fusion | bytes 96 | tf_op jit(solution)/shard_map/squeeze | solution.py:368
  56.5 1.9 %copy.14 = f32[1,8,16,1024]{3,2,1,0:T(8,128)} copy(f32[1,8,16,1024]{3,2,1,0:T(8,128)} %get-tuple-element.8) | data formatting | bytes 1048576

commit v2 on v1

--- a/solution.py
+++ b/solution.py
@@ -104,17 +104,17 @@
 
 
 def mixed(ref, vmix, level, count):
-    total = vmix[0, level, 0] * ref[0, 8:24, :]
+    total = vmix[level, 0] * ref[0, 8:24, :]
     for m in range(1, count):
-        total = total + vmix[0, level, m] * ref[m, 8:24, :]
+        total = total + vmix[level, m] * ref[m, 8:24, :]
     return total
 
 
 def kernel(
-    state, basis, kappa, land, slots, weights, vmix, rows, direction, coefs,
-    x0, x1, y, fh, f, basis_v, kap, land_v, maskf, surf, bucket, arrived, imp,
+    state, basis, kappa, land, slots_hbm, weights_hbm, vmix_hbm, rows_hbm, direction, coefs,
+    slots, weights, vmix, rows, x0, x1, y, fh, f, basis_v, kap, land_v, maskf, surf, bucket, arrived, imp,
     g_mine, g_pair, g_wide, g_part, g_other, e_mine, e_pair, e_wide, e_part, e_other,
-    load, send, recv, halo, gsem, esem, store,
+    load, send, recv, halo, gsem, esem,
 ):
     comp = lax.axis_index("comp")
     tile = lax.axis_index("tile")
@@ -130,6 +130,8 @@
     ]
     for c in surf_loads:
         c.start()
+    rows_load = pltpu.make_async_copy(rows_hbm.at[0, 0], rows, load.at[5])
+    rows_load.start()
     x_load = pltpu.make_async_copy(state.at[0], x0.at[:, pl.ds(8, ROWS), :], load.at[1])
     x_load.start()
     barrier = pltpu.get_barrier_semaphore()
@@ -145,10 +147,19 @@
     kap_load.start()
     land_load = pltpu.make_async_copy(land, land_v, load.at[3])
     land_load.start()
+    vmix_load = pltpu.make_async_copy(vmix_hbm.at[0], vmix, load.at[6])
+    vmix_load.start()
+    table_loads = [
+        pltpu.make_async_copy(slots_hbm.at[0, 0], slots, load.at[7]),
+        pltpu.make_async_copy(weights_hbm.at[0, 0], weights, load.at[8]),
+    ]
+    for c in table_loads:
+        c.start()
     basis_load = pltpu.make_async_copy(basis.at[:, 0], basis_v, load.at[4])
     basis_load.start()
     for c in surf_loads:
         c.wait()
+    rows_load.wait()
     x_load.wait()
     pl.semaphore_wait(barrier, TILES + 2)
 
@@ -178,7 +189,7 @@
     def deliver(step, carry):
         dest = moved_tile(tile, step)
         for j in range(CAP):
-            blk = rows[0, 0, dest, j]
+            blk = rows[j, dest]
             start = (blk & 7) * (FLUX * ROWS) + (blk >> 3)
             flat_bucket[pl.ds(step * (FLUX * CAP) + j, FLUX, stride=CAP), :] = flat_surf[
                 pl.ds(start, FLUX, stride=ROWS), :
@@ -219,6 +230,7 @@
     g_mine[...] = gram_here
 
     kap_load.wait()
+    vmix_load.wait()
     land_load.wait()
     maskf[...] = jnp.where(comp == 0, land_v[...].astype(F32), jnp.ones((ROWS, COLS), F32))
     for c in swap0:
@@ -234,17 +246,19 @@
     for l in range(LEV):
         y[l] = maskf[...] * (stencil(x1, l, kap[...]) + mixed(x1, vmix, l, LEV))
 
-    slot = slots[0, 0]
-    weight = weights[0, 0]
+    for c in table_loads:
+        c.wait()
+    slot = slots[...]
     src = slot >> 3
     a = (tile & 3) - (src & 3) & 3
     b = (tile >> 2 & 3) - (src >> 2 & 3) - a & 3
     c = (tile >> 4) - (src >> 4) - a & 3
     place = (a | b << 2 | c << 4) * CAP + (slot & 7)
-    at_lane = lax.broadcasted_iota(jnp.int32, (NB, TILES * CAP), 1)
+    table = jnp.concatenate([place.astype(F32), weights[...], jnp.zeros((NB - 8, NB), F32)], axis=0).T
+    at_lane = lax.broadcasted_iota(jnp.int32, (NB, TILES * CAP), 1).astype(F32)
     matrix = jnp.zeros((NB, TILES * CAP), F32)
     for k in range(4):
-        matrix = matrix + jnp.where(at_lane == place[:, k : k + 1], weight[:, k : k + 1], 0.0)
+        matrix = matrix + jnp.where(at_lane == table[:, k : k + 1], table[:, 4 + k : 5 + k], 0.0)
     high = matrix.astype(BF16)
     low = (matrix - high.astype(F32)).astype(BF16)
     dot = functools.partial(jnp.dot, preferred_element_type=F32)
@@ -289,7 +303,7 @@
     dots = sum_over_devices(comp, tile, e_mine, e_pair, e_wide, e_part, e_other, esem)
     first = lax.broadcasted_iota(jnp.int32, (1, 128), 1)
     coef = jnp.where(first < VECS, dots * (1.0 / total), 0.0)
-    coefs[...] = coef
+    coefs[...] = coef[0, :VECS]
     coef_col = jnp.sum(jnp.where(lane == sub, jnp.broadcast_to(coef, (16, 128)), 0.0), axis=1, keepdims=True)
     square = jnp.sum(jnp.where(first == VECS, dots, 0.0) - 2.0 * dots * coef, axis=1, keepdims=True)
     gc = jnp.sum(gram * coef, axis=1, keepdims=True)
@@ -305,30 +319,30 @@
             w = scale * y[l, :, pl.ds(at, 128)]
             for i in range(VECS):
                 w = w - weigh[i] * basis_v[i, l, :, pl.ds(at, 128)].astype(F32)
-            y[l, :, pl.ds(at, 128)] = w
+            direction[0, l, :, pl.ds(at, 128)] = w
             return carry
 
         lax.fori_loop(0, 8, finish, 0)
-        pltpu.make_async_copy(y.at[l], direction.at[0, l], store).start()
     wait_bytes(bucket, send)
-    wait_bytes(y, store)
 
 
 def body(state, basis, kappa, vmix, land_mask, send_rows, recv_slots, recv_weights):
-    anywhere = pl.BlockSpec(memory_space=pl.ANY)
     vmem = pl.BlockSpec(memory_space=pltpu.VMEM)
-    smem = pl.BlockSpec(memory_space=pltpu.SMEM)
     dma = pltpu.SemaphoreType.DMA
     pad = (LEV, 32, COLS)
-    direction, coefs = pl.pallas_call(
+    return pl.pallas_call(
         kernel,
         out_shape=(
             jax.ShapeDtypeStruct((1, LEV, ROWS, COLS), F32),
-            jax.ShapeDtypeStruct((1, 128), F32),
+            jax.ShapeDtypeStruct((VECS,), F32),
         ),
-        in_specs=[anywhere, anywhere, anywhere, anywhere, vmem, vmem, smem, smem],
-        out_specs=(anywhere, vmem),
+        in_specs=[pl.BlockSpec(memory_space=pltpu.HBM)] * 8,
+        out_specs=(vmem, vmem),
         scratch_shapes=[
+            pltpu.VMEM((4, NB), jnp.int32),
+            pltpu.VMEM((4, NB), F32),
+            pltpu.SMEM((LEV, LEV), F32),
+            pltpu.SMEM((CAP, TILES), jnp.int32),
             pltpu.VMEM(pad, F32),
             pltpu.VMEM(pad, F32),
             pltpu.VMEM((LEV, ROWS, COLS), F32),
@@ -352,20 +366,32 @@
             pltpu.VMEM((TILES // 2, 1, 128), F32),
             pltpu.VMEM((1, 128), F32),
             pltpu.VMEM((1, 128), F32),
-            dma((5,)),
+            dma((9,)),
             dma(()),
             dma((GROUPS,)),
             dma((3, 4)),
             dma((6,)),
             dma((6,)),
-            dma(()),
         ],
         compiler_params=pltpu.CompilerParams(
-            collective_id=0, has_side_effects=True, vmem_limit_bytes=56 << 20
+            collective_id=0, has_side_effects=True, vmem_limit_bytes=24 << 20
         ),
         name="interval",
-    )(state, basis, kappa, land_mask, recv_slots, recv_weights, vmix, send_rows)
-    return direction, coefs[0, :VECS]
+    )(
+        *(
+            pltpu.with_memory_space_constraint(v, pltpu.HBM)
+            for v in (
+                state,
+                basis,
+                kappa,
+                land_mask,
+                jnp.swapaxes(recv_slots, 2, 3),
+                jnp.swapaxes(recv_weights, 2, 3),
+                vmix,
+                jnp.swapaxes(send_rows, 2, 3),
+            )
+        )
+    )
 
 
 def solution(mesh):

time: 58.7 us -> 50.3 us (0.86)
  local copies, waits for them, and re-layouts: 7.22 us -> 1.31 us
  Pallas kernels: 50.5 us -> 48.3 us
    unnamed x4 -> x2, local copies, waits for them, and re-layouts: 6.11 us -> 1.31 us
    pallas_call x1, Pallas kernels: 50.5 us -> 48.3 us  [body(): pl.pallas_call(kernel, out_shape=(jax.ShapeDtypeStruct((1, LEV, ROWS, COL...]
    squeeze x1 -> x0, local copies, waits for them, and re-layouts: 1.11 us -> none  [body(): return (direction, coefs[0, :VECS])]
where the time goes in v2:
time: 50.3 us; the launch traced here: 50.2 us
  Pallas kernels  48.3 us (96%)
  local copies, waits for them, and re-layouts  1.31 us (3%)
  between operations  0.64 us (1%)
    pallas_call x1, Pallas kernels, body(): pl.pallas_call(kernel, out_shape=(jax.ShapeDtypeStruct((1, LEV, ROWS, COL...  48.3 us
    unnamed x2, local copies, waits for them, and re-layouts  1.31 us

profile of v2, /device:TPU:1, one launch (start us, length us, event | category | flops | bytes accessed | tf_op | source)
XLA Modules:
  0.0 50.2 jit_solution(14199769425230312720)
XLA Ops:
  0.6 48.3 %interval.1 = (f32[1,8,16,1024]{3,2,1,0:T(8,128)S(1)}, f32[12]{0:T(128)S(1)}) custom-call(f32[1,8,16,1024]{3,2,1,0:T(8,128)} %state.1, bf16[12,1,8,16,1024]{4,3,2,1,0:T(8,128)(2,1)} %basis.1, f32[1,16,1024]{2,1,0:T(8,128)} %kappa.1, s32[16,1024]{1,0:T(8,128)} %land.1, s32[1,1,4,128]{3,2,1,0:T(4,128)} %bitcast.4, f32[1,1,4,128]{3,2,1,0:T(4,128)} %bitcast.5, ...), custom_call_target="tpu_custom_call" | custom-call | tf_op jit(solution)/shard_map/interval/pallas_call | solution.py:333
  48.9 0.8 %copy.12 = f32[1,8,16,1024]{3,2,1,0:T(8,128)} copy(f32[1,8,16,1024]{3,2,1,0:T(8,128)S(1)} %get-tuple-element.4) | data formatting | bytes 1048576
  49.7 0.5 %copy.13 = f32[12]{0:T(128)} copy(f32[12]{0:T(128)S(1)} %get-tuple-element.5) | data formatting | bytes 96

commit v3 on v2

v3 whole, which is shorter than its diff:
```python
import functools

import jax
import jax.numpy as jnp
from jax import lax
from jax.experimental import pallas as pl
from jax.experimental.pallas import tpu as pltpu
from jax.sharding import PartitionSpec as P

FLUX = 4
VECS = 12
LEV = 8
ROWS = 16
COLS = 1024
TILES = 64
CAP = 8
NB = 128
GROUPS = 4
PER = TILES // GROUPS
MESH = pl.DeviceIdType.MESH
F32 = jnp.float32
BF16 = jnp.bfloat16
PAIRS = [(k, i, (i + k) % VECS) for k in range(VECS // 2 + 1) for i in range(VECS if k < VECS // 2 else VECS // 2)]
SEG = 16


def hops(k):
    return sum((0, 1, 2, 1)[(k >> s) & 3] for s in (0, 2, 4))


PEERS = [sorted((k for k in range(1, TILES) if k & 1 == c), key=lambda k: -hops(k)) for c in (0, 1)]


def offset_of(step):
    a, b, c = step & 3, (step >> 2) & 3, step >> 4
    return a, (a + b) & 3, (a + c) & 3


def moved_tile(tile, step):
    dx, dy, dz = offset_of(step)
    return ((tile & 3) + dx & 3) | (((tile >> 2 & 3) + dy & 3) << 2) | (((tile >> 4) + dz & 3) << 4)


def remote(src, dst, send, recv, comp, tile):
    return pltpu.make_async_remote_copy(
        src_ref=src, dst_ref=dst, send_sem=send, recv_sem=recv, device_id=(comp, tile), device_id_type=MESH
    )


def wait_bytes(ref, sem):
    pltpu.make_async_copy(ref, ref, sem).wait()


def sum_over_devices(comp, tile, mine, pair, wide, part, other, sems, meanwhile):
    first = remote(mine, pair, sems.at[0], sems.at[1], 1 - comp, tile)
    first.start()
    first.wait()
    chip = mine[...] + pair[...]
    part[...] = chip
    odd = tile & 1
    slot = tile >> 1

    for c in (0, 1):

        @pl.when(comp == c)
        def _():
            for k in PEERS[c]:
                remote(part, wide.at[slot], sems.at[2], sems.at[3], odd, tile ^ k).start()

    meanwhile()

    @pl.when(comp == odd)
    def _():
        wide[slot] = chip
        wait_bytes(wide.at[pl.ds(0, TILES // 2 - 1)], sems.at[3])

    @pl.when(comp != odd)
    def _():
        wait_bytes(wide.at[pl.ds(0, TILES // 2)], sems.at[3])

    half = wide[0]
    for s in range(1, TILES // 2):
        half = half + wide[s]
    for c in (0, 1):

        @pl.when(comp == c)
        def _():
            wait_bytes(wide.at[pl.ds(0, len(PEERS[c]))], sems.at[2])

    part[...] = half
    last = remote(part, other, sems.at[4], sems.at[5], 1 - comp, tile)
    last.start()
    last.wait()
    return half + other[...]


def stencil(ref, level, kap, row, count):
    x = ref[level, row : row + count, :]
    lap = (
        ref[level, row - 1 : row - 1 + count, :]
        + ref[level, row + 1 : row + 1 + count, :]
        + pltpu.roll(x, 1, 1)
        + pltpu.roll(x, COLS - 1, 1)
        - 4.0 * x
    )
    return x + kap * lap


def mixed(ref, vmix, level, terms, row, count):
    total = vmix[level, 0] * ref[0, row : row + count, :]
    for m in range(1, terms):
        total = total + vmix[level, m] * ref[m, row : row + count, :]
    return total


def kernel(
    state, basis, kappa, land, slots_hbm, weights_hbm, vmix_hbm, rows_hbm,
    x2, basis_v, result,
    slots, weights, vmix, rows, x0, x1, fh, f, kap, land_v, maskf, kap_far, land_far,
    surf, bucket, arrived, imp, edge_b, edge_out, edge_in, edge_k, edge_m, near,
    e_mine, e_pair, e_wide, e_part, e_other,
    load, send, recv, halo, esem,
):
    comp = lax.axis_index("comp")
    tile = lax.axis_index("tile")
    total = float(LEV * ROWS * COLS * TILES * 2)
    above = tile - 1 & TILES - 1
    below = tile + 1 & TILES - 1
    every = range(8)

    surf_loads = [
        pltpu.make_async_copy(
            state.at[0, pl.ds(0, FLUX), :, pl.ds(128 * j, 128)], surf.at[j], load.at[0]
        )
        for j in every
    ]
    for c in surf_loads:
        c.start()
    rows_load = pltpu.make_async_copy(rows_hbm.at[0, 0], rows, load.at[5])
    rows_load.start()
    x_load = pltpu.make_async_copy(state.at[0], x0.at[:, pl.ds(8, ROWS), :], load.at[1])
    x_load.start()
    kap_load = pltpu.make_async_copy(kappa.at[0], kap, load.at[2])
    kap_load.start()
    land_load = pltpu.make_async_copy(land, land_v, load.at[3])
    land_load.start()
    barrier = pltpu.get_barrier_semaphore()

    def greet(step, carry):
        pl.semaphore_signal(barrier, inc=1, device_id=(1 - comp, moved_tile(tile, step)), device_id_type=MESH)
        return carry

    lax.fori_loop(0, TILES, greet, 0)
    for t in (above, below):
        pl.semaphore_signal(barrier, inc=1, device_id=(comp, t), device_id_type=MESH)
    vmix_load = pltpu.make_async_copy(vmix_hbm.at[0], vmix, load.at[6])
    vmix_load.start()
    table_loads = [
        pltpu.make_async_copy(slots_hbm.at[0, 0], slots, load.at[7]),
        pltpu.make_async_copy(weights_hbm.at[0, 0], weights, load.at[8]),
    ]
    for c in table_loads:
        c.start()
    basis_load = pltpu.make_async_copy(basis.at[:, 0], basis_v, load.at[4])
    basis_load.start()
    for c in surf_loads:
        c.wait()
    rows_load.wait()
    x_load.wait()
    kap_load.wait()
    land_load.wait()
    pl.semaphore_wait(barrier, TILES + 2)

    swaps = [
        remote(x0.at[:, pl.ds(8, 2), :], x0.at[:, pl.ds(24, 2), :], halo.at[0], halo.at[1], comp, above),
        remote(x0.at[:, pl.ds(22, 2), :], x0.at[:, pl.ds(6, 2), :], halo.at[2], halo.at[3], comp, below),
        remote(kap.at[pl.ds(0, 1)], kap_far.at[1], halo.at[4], halo.at[5], comp, above),
        remote(kap.at[pl.ds(15, 1)], kap_far.at[0], halo.at[6], halo.at[7], comp, below),
        remote(land_v.at[pl.ds(0, 1)], land_far.at[1], halo.at[8], halo.at[9], comp, above),
        remote(land_v.at[pl.ds(15, 1)], land_far.at[0], halo.at[10], halo.at[11], comp, below),
    ]
    for c in swaps:
        c.start()

    flat_surf = surf.reshape(8 * FLUX * ROWS, 128)
    flat_bucket = bucket.reshape(TILES * FLUX * CAP, 128)

    def deliver(step, carry):
        dest = moved_tile(tile, step)
        for j in range(CAP):
            blk = rows[j, dest]
            start = (blk & 7) * (FLUX * ROWS) + (blk >> 3)
            flat_bucket[pl.ds(step * (FLUX * CAP) + j, FLUX, stride=CAP), :] = flat_surf[
                pl.ds(start, FLUX, stride=ROWS), :
            ]
        remote(bucket.at[step], arrived.at[step], send, recv.at[step >> 4], 1 - comp, dest).start()
        return carry

    lax.fori_loop(0, TILES, deliver, 0)

    vmix_load.wait()
    maskf[...] = jnp.where(comp == 0, land_v[...].astype(F32), jnp.ones((ROWS, COLS), F32))
    for c in swaps:
        c.wait()

    @pl.when(tile == 0)
    def _():
        x0[:, 6:8, :] = jnp.zeros((LEV, 2, COLS), F32)

    @pl.when(tile == TILES - 1)
    def _():
        x0[:, 24:26, :] = jnp.zeros((LEV, 2, COLS), F32)

    for l in range(LEV):
        x1[l, 8:24, :] = maskf[...] * (stencil(x0, l, kap[...], 8, ROWS) + mixed(x0, vmix, l, LEV, 8, ROWS))
    for end, row, last in ((0, 7, 0), (1, 24, TILES - 1)):
        far = jnp.where(comp == 0, land_far[end].astype(F32), jnp.ones((1, COLS), F32))
        far = jnp.where(tile == last, jnp.zeros((1, COLS), F32), far)
        for l in range(LEV):
            x1[l, row : row + 1, :] = far * (
                stencil(x0, l, kap_far[end], row, 1) + mixed(x0, vmix, l, LEV, row, 1)
            )
    for l in range(LEV):
        x2[l] = maskf[...] * (stencil(x1, l, kap[...], 8, ROWS) + mixed(x1, vmix, l, LEV, 8, ROWS))

    for j in every:
        cut = slice(j * 128, (j + 1) * 128)
        for end, row in ((0, 0), (1, 15)):
            m = maskf[row : row + 1, cut]
            edge_m[end, j : j + 1] = m
            edge_k[end, j : j + 1] = m * kap[row : row + 1, cut]
    fh[:, 7:8, :] = jnp.zeros((FLUX, 1, COLS), F32)
    fh[:, 24:25, :] = jnp.zeros((FLUX, 1, COLS), F32)

    for c in table_loads:
        c.wait()
    slot = slots[...]
    src = slot >> 3
    a = (tile & 3) - (src & 3) & 3
    b = (tile >> 2 & 3) - (src >> 2 & 3) - a & 3
    c = (tile >> 4) - (src >> 4) - a & 3
    place = (a | b << 2 | c << 4) * CAP + (slot & 7)
    table = jnp.concatenate([place.astype(F32), weights[...], jnp.zeros((NB - 8, NB), F32)], axis=0).T
    at_lane = lax.broadcasted_iota(jnp.int32, (NB, TILES * CAP), 1).astype(F32)
    matrix = jnp.zeros((NB, TILES * CAP), F32)
    for k in range(4):
        matrix = matrix + jnp.where(at_lane == table[:, k : k + 1], table[:, 4 + k : 5 + k], 0.0)
    ends = jnp.concatenate([matrix[:8], matrix[-8:]], axis=0)

    def halves(v):
        high = v.astype(BF16)
        return high, (v - high.astype(F32)).astype(BF16)

    high, low = halves(matrix)
    ends_high, ends_low = halves(ends)

    basis_load.wait()
    lane = lax.broadcasted_iota(jnp.int32, (SEG, 128), 1)
    sub = lax.broadcasted_iota(jnp.int32, (SEG, 128), 0)
    rows_of = {}
    third = len(PAIRS) // 3
    for part in range(3):
        pairs = PAIRS[part * third : (part + 1) * third]

        def gram_step(n, acc, pairs=pairs):
            level = n >> 3
            at = pl.multiple_of((n & 7) * 128, 128)
            used = sorted({i for p in pairs for i in p[1:]})
            vals = {i: basis_v[i, level, :, pl.ds(at, 128)].astype(F32) for i in used}
            out = []
            for (_, i, j), a in zip(pairs, acc):
                p = vals[i] * vals[j]
                out.append(a + (p[:8] + p[8:]))
            return tuple(out)

        acc = lax.fori_loop(0, 64, gram_step, tuple(jnp.zeros((8, 128), F32) for _ in pairs))
        for (k, i, _), a in zip(pairs, acc):
            rows_of[k, i] = jnp.sum(a, axis=0, keepdims=True)
    empty = jnp.zeros((1, 128), F32)

    def to_lanes(rows_, k):
        stack = jnp.concatenate(rows_ + [empty] * (SEG - len(rows_)), axis=0)
        return jnp.where(lane == sub + SEG * k, jnp.sum(stack, axis=1, keepdims=True), 0.0)

    gram = jnp.zeros((SEG, 128), F32)
    for k in range(VECS // 2 + 1):
        gram = gram + to_lanes([rows_of[k, i] for i in range(VECS) if (k, i) in rows_of], k)

    def edge_step(i, carry):
        for l in range(FLUX):
            for j in every:
                v = basis_v[i, l, :, j * 128 : (j + 1) * 128].astype(F32)
                edge_b[i, l, 0, j : j + 1] = v[:1]
                edge_b[i, l, 1, j : j + 1] = v[15:]
        return carry

    lax.fori_loop(0, VECS, edge_step, 0)

    dot = functools.partial(jnp.dot, preferred_element_type=F32)

    def group(g):
        wait_bytes(arrived.at[pl.ds(g * PER, PER)], recv.at[g])
        got = jnp.concatenate(
            [arrived[g * PER : (g + 1) * PER, i].reshape(PER * CAP, 128) for i in range(FLUX)], axis=1
        )
        return slice(g * PER * CAP, (g + 1) * PER * CAP), *halves(got)

    def times(high, low, cut, got_high, got_low):
        return dot(high[:, cut], got_high) + dot(low[:, cut], got_high) + dot(high[:, cut], got_low)

    sums = jnp.zeros((NB, FLUX * 128), F32)
    for g in range(GROUPS - 1):
        sums = sums + times(high, low, *group(g))
    tail = group(GROUPS - 1)
    border = jnp.concatenate([sums[:8], sums[-8:]], axis=0) + times(ends_high, ends_low, *tail)
    for end in (0, 1):
        for i in range(FLUX):
            edge_out[end, i] = edge_m[end] * border[end * 8 : end * 8 + 8, i * 128 : (i + 1) * 128]
    edges = [
        remote(edge_out.at[0], edge_in.at[1], halo.at[12], halo.at[13], comp, above),
        remote(edge_out.at[1], edge_in.at[0], halo.at[14], halo.at[15], comp, below),
    ]
    for c in edges:
        c.start()
    sums = sums + times(high, low, *tail)
    for i in range(FLUX):
        imp[i * NB : (i + 1) * NB, :] = sums[:, i * 128 : (i + 1) * 128]
    for i in range(FLUX):
        for j in every:
            cut = slice(j * 128, (j + 1) * 128)
            piece = imp[pl.ds(i * NB + j, ROWS, stride=8), :]
            f[i, :, cut] = piece
            fh[i, 8:24, cut] = maskf[:, cut] * piece
    for l in range(LEV):
        z = mixed(fh, vmix, l, FLUX, 8, ROWS)
        if l < FLUX:
            z = z + stencil(fh, l, kap[...], 8, ROWS) + f[l]
        x2[l] = x2[l] + maskf[...] * z

    def dot_step(n, acc):
        level = n >> 2
        for half in (0, 1):
            at = pl.multiple_of((n & 3) * 256 + half * 128, 128)
            x = x2[level, :, pl.ds(at, 128)]
            out = [a + basis_v[i, level, :, pl.ds(at, 128)].astype(F32) * x for i, a in enumerate(acc[:VECS])]
            acc = tuple(out) + (acc[VECS] + x * x,)
        return acc

    acc = lax.fori_loop(0, 32, dot_step, tuple(jnp.zeros((16, 128), F32) for _ in range(VECS + 1)))
    acc = [a[:8] + a[8:] for a in acc]
    for l in range(FLUX):
        for end, row in ((0, 0), (1, 15)):
            for j in every:
                near[l, end, j : j + 1] = x2[l, row : row + 1, j * 128 : (j + 1) * 128]
    for c in edges:
        c.wait()
    extra = {}
    for end, last in ((0, 0), (1, TILES - 1)):
        factor = jnp.where(tile == last, jnp.zeros((8, 128), F32), edge_k[end])
        for l in range(FLUX):
            add = factor * edge_in[end, l]
            extra[l, end] = add
            for i in range(VECS):
                acc[i] = acc[i] + edge_b[i, l, end] * add
            acc[VECS] = acc[VECS] + add * (2.0 * near[l, end] + add)
    sums_of = [jnp.sum(a, axis=0, keepdims=True) for a in acc]
    e_mine[...] = jnp.sum(gram + to_lanes(sums_of, 7), axis=0, keepdims=True)

    def add_edges():
        for (l, end), add in extra.items():
            row = 15 * end
            full = near[l, end] + add
            for j in every:
                x2[l, row : row + 1, j * 128 : (j + 1) * 128] = full[j : j + 1]

    dots = sum_over_devices(comp, tile, e_mine, e_pair, e_wide, e_part, e_other, esem, add_edges)

    one = lax.broadcasted_iota(jnp.int32, (1, 128), 1)
    seg, pos = one >> 4, one & 15
    vals = jnp.where((seg == 7) & (pos < VECS), dots * (1.0 / total), 0.0)
    coef = pltpu.roll(vals, SEG, 1)
    twice = coef + pltpu.roll(coef, VECS, 1)
    left = jnp.zeros((1, 128), F32)
    right = jnp.zeros((1, 128), F32)
    for k in range(VECS // 2 + 1):
        left = jnp.where(seg == k, pltpu.roll(coef, SEG * k, 1) if k else coef, left)
        right = jnp.where(seg == k, pltpu.roll(twice, (SEG - 1) * k, 1) if k else twice, right)
    factor = jnp.where(seg == 0, 1.0, 2.0)
    products = jnp.where((seg < 7) & (pos < VECS), factor * dots * left * right, 0.0)
    square = jnp.where((seg == 7) & (pos == VECS), dots, 0.0) - 2.0 * dots * vals + products
    square = jnp.sum(square, axis=1, keepdims=True)
    scale = 1.0 / jnp.sqrt(jnp.maximum(square, 0.0) * (1.0 / total) + 1e-06)
    line = jnp.where(one == VECS, 1.0, coef)
    column = jnp.sum(jnp.where(lane == sub, jnp.broadcast_to(line, (SEG, 128)), 0.0), axis=1, keepdims=True)
    result[0:SEG] = jnp.broadcast_to(column * scale, (SEG, 128))
    result[SEG : SEG + 1] = coef
    wait_bytes(bucket, send)


def finish(x2, basis_v, result, direction, coefs, out, store):
    coefs[...] = result[SEG, :VECS]
    for l in range(LEV):

        def part(n, carry):
            at = pl.multiple_of(n * 128, 128)
            w = result[VECS : VECS + 1] * x2[l, :, pl.ds(at, 128)]
            for i in range(VECS):
                w = w - result[i : i + 1] * basis_v[i, l, :, pl.ds(at, 128)].astype(F32)
            out[l, :, pl.ds(at, 128)] = w
            return carry

        lax.fori_loop(0, 8, part, 0)
        pltpu.make_async_copy(out.at[l], direction.at[0, l], store).start()
    wait_bytes(out, store)


def body(state, basis, kappa, vmix, land_mask, send_rows, recv_slots, recv_weights):
    vmem = pl.BlockSpec(memory_space=pltpu.VMEM)
    dma = pltpu.SemaphoreType.DMA
    pad = (LEV, 32, COLS)
    band = (ROWS, COLS)
    ints = jnp.int32
    scratch = [((4, NB), ints), ((4, NB), F32), None, None, (pad, F32), (pad, F32)]
    scratch += [((FLUX, 32, COLS), F32), ((FLUX, ROWS, COLS), F32), (band, F32), (band, ints), (band, F32)]
    scratch += [((2, 1, COLS), F32), ((2, 1, COLS), ints), ((8, FLUX, ROWS, 128), F32)]
    scratch += [((TILES, FLUX, CAP, 128), F32)] * 2 + [((FLUX * NB, 128), F32)]
    scratch += [((VECS, FLUX, 2, 8, 128), F32)] + [((2, FLUX, 8, 128), F32)] * 2 + [((2, 8, 128), F32)] * 2
    scratch += [((FLUX, 2, 8, 128), F32)]
    scratch += [((1, 128), F32)] * 2 + [((TILES // 2, 1, 128), F32)] + [((1, 128), F32)] * 2
    scratch = [pltpu.VMEM(*v) if v else None for v in scratch]
    scratch[2] = pltpu.SMEM((LEV, LEV), F32)
    scratch[3] = pltpu.SMEM((CAP, TILES), ints)
    x2, basis_v, result = pl.pallas_call(
        kernel,
        out_shape=(
            jax.ShapeDtypeStruct((LEV, ROWS, COLS), F32),
            jax.ShapeDtypeStruct((VECS, LEV, ROWS, COLS), BF16),
            jax.ShapeDtypeStruct((SEG + 8, 128), F32),
        ),
        in_specs=[pl.BlockSpec(memory_space=pltpu.HBM)] * 8,
        out_specs=(vmem,) * 3,
        scratch_shapes=scratch + [dma((9,)), dma(()), dma((GROUPS,)), dma((16,)), dma((6,))],
        compiler_params=pltpu.CompilerParams(
            collective_id=0, has_side_effects=True, vmem_limit_bytes=24 << 20
        ),
        name="interval",
    )(
        *(
            pltpu.with_memory_space_constraint(v, pltpu.HBM)
            for v in (
                state,
                basis,
                kappa,
                land_mask,
                jnp.swapaxes(recv_slots, 2, 3),
                jnp.swapaxes(recv_weights, 2, 3),
                vmix,
                jnp.swapaxes(send_rows, 2, 3),
            )
        )
    )
    return pl.pallas_call(
        finish,
        out_shape=(
            jax.ShapeDtypeStruct((1, LEV, ROWS, COLS), F32),
            jax.ShapeDtypeStruct((VECS,), F32),
        ),
        in_specs=[vmem] * 3,
        out_specs=(pl.BlockSpec(memory_space=pl.ANY), vmem),
        scratch_shapes=[pltpu.VMEM((LEV, ROWS, COLS), F32), dma(())],
        compiler_params=pltpu.CompilerParams(vmem_limit_bytes=16 << 20),
        name="finish",
    )(x2, basis_v, result)


def solution(mesh):
    return jax.shard_map(
        body,
        mesh=mesh,
        in_specs=(
            P("comp", None, "tile", None),
            P(None, "comp", None, "tile", None),
            P("comp", "tile", None),
            P("comp", None, None),
            P("tile", None),
            P("comp", "tile", None, None),
            P("comp", "tile", None, None),
            P("comp", "tile", None, None),
        ),
        out_specs=(P("comp", None, "tile", None), P()),
        check_vma=False,
    )
```

time: 50.3 us -> 43.8 us (0.87)
  Pallas kernels: 48.3 us -> 43.1 us
  local copies, waits for them, and re-layouts: 1.31 us -> 0 us
    pallas_call x1 -> x2, Pallas kernels: 48.3 us -> 43.1 us  [the longest x1 40.6 us: body(): pl.pallas_call(kernel, out_shape=(jax.ShapeDtypeStruct((LEV, ROWS, COLS),...]
    unnamed x2 -> x0, local copies, waits for them, and re-layouts: 1.31 us -> none
where the time goes in v3:
time: 43.8 us; the launch traced here: 43.7 us
  Pallas kernels  43.1 us (98%)
  between operations  0.64 us (1%)
    pallas_call x1, Pallas kernels, body(): pl.pallas_call(kernel, out_shape=(jax.ShapeDtypeStruct((LEV, ROWS, COLS),...  40.6 us
    pallas_call x1, Pallas kernels, body(): pl.pallas_call(finish, out_shape=(jax.ShapeDtypeStruct((1, LEV, ROWS, COL...  2.52 us

profile of v3, /device:TPU:1, one launch (start us, length us, event | category | flops | bytes accessed | tf_op | source)
XLA Modules:
  0.0 43.7 jit_solution(17230332058844905478)
XLA Ops:
  0.6 40.6 %interval.1 = (f32[8,16,1024]{2,1,0:T(8,128)S(1)}, bf16[12,8,16,1024]{3,2,1,0:T(8,128)(2,1)S(1)}, f32[24,128]{1,0:T(8,128)S(1)}) custom-call(f32[1,8,16,1024]{3,2,1,0:T(8,128)} %state.1, bf16[12,1,8,16,1024]{4,3,2,1,0:T(8,128)(2,1)} %basis.1, f32[1,16,1024]{2,1,0:T(8,128)} %kappa.1, s32[16,1024]{1,0:T(8,128)} %land.1, s32[1,1,4,128]{3,2,1,0:T(4,128)} %bitcast.4, ...), custom_call_target="tpu_custom_call" | custom-call | tf_op jit(solution)/shard_map/interval/pallas_call | solution.py:433
  41.2 2.5 %finish.1 = (f32[1,8,16,1024]{3,2,1,0:T(8,128)}, f32[12]{0:T(128)}) custom-call(f32[8,16,1024]{2,1,0:T(8,128)S(1)} %get-tuple-element.5.x2, bf16[12,8,16,1024]{3,2,1,0:T(8,128)(2,1)S(1)} %get-tuple-element.6.basis_v, f32[24,128]{1,0:T(8,128)S(1)} %get-tuple-element.7.result), custom_call_target="tpu_custom_call" | custom-call | tf_op jit(solution)/shard_map/finish/pallas_call | solution.py:462

commit v4 on v3

--- a/solution.py
+++ b/solution.py
@@ -20,7 +20,6 @@
 MESH = pl.DeviceIdType.MESH
 F32 = jnp.float32
 BF16 = jnp.bfloat16
-PAIRS = [(k, i, (i + k) % VECS) for k in range(VECS // 2 + 1) for i in range(VECS if k < VECS // 2 else VECS // 2)]
 SEG = 16
 
 
@@ -28,12 +27,15 @@
     return sum((0, 1, 2, 1)[(k >> s) & 3] for s in (0, 2, 4))
 
 
+FAR_FIRST = sorted(range(TILES), key=lambda k: -hops(k))
+
+
 PEERS = [sorted((k for k in range(1, TILES) if k & 1 == c), key=lambda k: -hops(k)) for c in (0, 1)]
 
 
 def offset_of(step):
     a, b, c = step & 3, (step >> 2) & 3, step >> 4
-    return a, (a + b) & 3, (a + c) & 3
+    return a, (b - a) & 3, (a + c) & 3
 
 
 def moved_tile(tile, step):
@@ -94,11 +96,11 @@
     return half + other[...]
 
 
-def stencil(ref, level, kap, row, count):
-    x = ref[level, row : row + count, :]
+def stencil(ref, level, kap):
+    x = ref[level, 8:24, :]
     lap = (
-        ref[level, row - 1 : row - 1 + count, :]
-        + ref[level, row + 1 : row + 1 + count, :]
+        ref[level, 7:23, :]
+        + ref[level, 9:25, :]
         + pltpu.roll(x, 1, 1)
         + pltpu.roll(x, COLS - 1, 1)
         - 4.0 * x
@@ -106,17 +108,17 @@
     return x + kap * lap
 
 
-def mixed(ref, vmix, level, terms, row, count):
-    total = vmix[level, 0] * ref[0, row : row + count, :]
+def mixed(ref, vmix, level, terms):
+    total = vmix[level, 0] * ref[0, 8:24, :]
     for m in range(1, terms):
-        total = total + vmix[level, m] * ref[m, row : row + count, :]
+        total = total + vmix[level, m] * ref[m, 8:24, :]
     return total
 
 
 def kernel(
     state, basis, kappa, land, slots_hbm, weights_hbm, vmix_hbm, rows_hbm,
     x2, basis_v, result,
-    slots, weights, vmix, rows, x0, x1, fh, f, kap, land_v, maskf, kap_far, land_far,
+    slots, weights, vmix, rows, x0, x1, fh, f, kap, land_v, maskf, gram_v, edge_x,
     surf, bucket, arrived, imp, edge_b, edge_out, edge_in, edge_k, edge_m, near,
     e_mine, e_pair, e_wide, e_part, e_other,
     load, send, recv, halo, esem,
@@ -128,31 +130,30 @@
     below = tile + 1 & TILES - 1
     every = range(8)
 
+    barrier = pltpu.get_barrier_semaphore()
+
+    def greet(ks):
+        for k in ks:
+            pl.semaphore_signal(barrier, inc=1, device_id=(1 - comp, tile ^ k), device_id_type=MESH)
+
+    greet(FAR_FIRST[:32])
     surf_loads = [
         pltpu.make_async_copy(
             state.at[0, pl.ds(0, FLUX), :, pl.ds(128 * j, 128)], surf.at[j], load.at[0]
         )
         for j in every
     ]
-    for c in surf_loads:
+    rows_load = pltpu.make_async_copy(rows_hbm.at[0, 0], rows, load.at[5])
+    x_load = pltpu.make_async_copy(state.at[0], x0.at[:, pl.ds(8, ROWS), :], load.at[1])
+    for c in [rows_load, x_load, *surf_loads]:
         c.start()
-    rows_load = pltpu.make_async_copy(rows_hbm.at[0, 0], rows, load.at[5])
-    rows_load.start()
-    x_load = pltpu.make_async_copy(state.at[0], x0.at[:, pl.ds(8, ROWS), :], load.at[1])
-    x_load.start()
+    greet(FAR_FIRST[32:])
+    for t in (above, below):
+        pl.semaphore_signal(barrier, inc=1, device_id=(comp, t), device_id_type=MESH)
     kap_load = pltpu.make_async_copy(kappa.at[0], kap, load.at[2])
     kap_load.start()
     land_load = pltpu.make_async_copy(land, land_v, load.at[3])
     land_load.start()
-    barrier = pltpu.get_barrier_semaphore()
-
-    def greet(step, carry):
-        pl.semaphore_signal(barrier, inc=1, device_id=(1 - comp, moved_tile(tile, step)), device_id_type=MESH)
-        return carry
-
-    lax.fori_loop(0, TILES, greet, 0)
-    for t in (above, below):
-        pl.semaphore_signal(barrier, inc=1, device_id=(comp, t), device_id_type=MESH)
     vmix_load = pltpu.make_async_copy(vmix_hbm.at[0], vmix, load.at[6])
     vmix_load.start()
     table_loads = [
@@ -163,24 +164,33 @@
         c.start()
     basis_load = pltpu.make_async_copy(basis.at[:, 0], basis_v, load.at[4])
     basis_load.start()
+    rows_load.wait()
+    x_load.wait()
     for c in surf_loads:
         c.wait()
-    rows_load.wait()
-    x_load.wait()
-    kap_load.wait()
-    land_load.wait()
     pl.semaphore_wait(barrier, TILES + 2)
 
-    swaps = [
-        remote(x0.at[:, pl.ds(8, 2), :], x0.at[:, pl.ds(24, 2), :], halo.at[0], halo.at[1], comp, above),
-        remote(x0.at[:, pl.ds(22, 2), :], x0.at[:, pl.ds(6, 2), :], halo.at[2], halo.at[3], comp, below),
-        remote(kap.at[pl.ds(0, 1)], kap_far.at[1], halo.at[4], halo.at[5], comp, above),
-        remote(kap.at[pl.ds(15, 1)], kap_far.at[0], halo.at[6], halo.at[7], comp, below),
-        remote(land_v.at[pl.ds(0, 1)], land_far.at[1], halo.at[8], halo.at[9], comp, above),
-        remote(land_v.at[pl.ds(15, 1)], land_far.at[0], halo.at[10], halo.at[11], comp, below),
-    ]
-    for c in swaps:
-        c.start()
+    def swap_rows(ref, sems):
+        pair = [
+            remote(ref.at[:, pl.ds(8, 1), :], ref.at[:, pl.ds(24, 1), :], sems.at[0], sems.at[1], comp, above),
+            remote(ref.at[:, pl.ds(23, 1), :], ref.at[:, pl.ds(7, 1), :], sems.at[2], sems.at[3], comp, below),
+        ]
+        for c in pair:
+            c.start()
+        return pair
+
+    def clear_ends(ref):
+        n = ref.shape[0]
+
+        @pl.when(tile == 0)
+        def _():
+            ref[:, 7:8, :] = jnp.zeros((n, 1, COLS), F32)
+
+        @pl.when(tile == TILES - 1)
+        def _():
+            ref[:, 24:25, :] = jnp.zeros((n, 1, COLS), F32)
+
+    swap = swap_rows(x0, halo.at[0])
 
     flat_surf = surf.reshape(8 * FLUX * ROWS, 128)
     flat_bucket = bucket.reshape(TILES * FLUX * CAP, 128)
@@ -196,32 +206,23 @@
         remote(bucket.at[step], arrived.at[step], send, recv.at[step >> 4], 1 - comp, dest).start()
         return carry
 
-    lax.fori_loop(0, TILES, deliver, 0)
+    lax.fori_loop(0, TILES // 2, deliver, 0)
 
     vmix_load.wait()
+    kap_load.wait()
+    land_load.wait()
     maskf[...] = jnp.where(comp == 0, land_v[...].astype(F32), jnp.ones((ROWS, COLS), F32))
-    for c in swaps:
+    for c in swap:
         c.wait()
-
-    @pl.when(tile == 0)
-    def _():
-        x0[:, 6:8, :] = jnp.zeros((LEV, 2, COLS), F32)
-
-    @pl.when(tile == TILES - 1)
-    def _():
-        x0[:, 24:26, :] = jnp.zeros((LEV, 2, COLS), F32)
-
+    clear_ends(x0)
     for l in range(LEV):
-        x1[l, 8:24, :] = maskf[...] * (stencil(x0, l, kap[...], 8, ROWS) + mixed(x0, vmix, l, LEV, 8, ROWS))
-    for end, row, last in ((0, 7, 0), (1, 24, TILES - 1)):
-        far = jnp.where(comp == 0, land_far[end].astype(F32), jnp.ones((1, COLS), F32))
-        far = jnp.where(tile == last, jnp.zeros((1, COLS), F32), far)
-        for l in range(LEV):
-            x1[l, row : row + 1, :] = far * (
-                stencil(x0, l, kap_far[end], row, 1) + mixed(x0, vmix, l, LEV, row, 1)
-            )
-    for l in range(LEV):
-        x2[l] = maskf[...] * (stencil(x1, l, kap[...], 8, ROWS) + mixed(x1, vmix, l, LEV, 8, ROWS))
+        x1[l, 8:24, :] = maskf[...] * (stencil(x0, l, kap[...]) + mixed(x0, vmix, l, LEV))
+    deep = x1.at[pl.ds(FLUX, LEV - FLUX)]
+    for row in (7, 24):
+        x1[0:FLUX, row : row + 1, :] = jnp.zeros((FLUX, 1, COLS), F32)
+        fh[:, row : row + 1, :] = jnp.zeros((FLUX, 1, COLS), F32)
+    swap = swap_rows(deep, halo.at[1])
+    lax.fori_loop(TILES // 2, TILES, deliver, 0)
 
     for j in every:
         cut = slice(j * 128, (j + 1) * 128)
@@ -229,15 +230,17 @@
             m = maskf[row : row + 1, cut]
             edge_m[end, j : j + 1] = m
             edge_k[end, j : j + 1] = m * kap[row : row + 1, cut]
-    fh[:, 7:8, :] = jnp.zeros((FLUX, 1, COLS), F32)
-    fh[:, 24:25, :] = jnp.zeros((FLUX, 1, COLS), F32)
+            for l in range(FLUX):
+                edge_x[end, l, j : j + 1] = x1[l, 8 + row : 9 + row, cut]
+    for l in range(FLUX):
+        x2[l] = maskf[...] * (stencil(x1, l, kap[...]) + mixed(x1, vmix, l, LEV))
 
     for c in table_loads:
         c.wait()
     slot = slots[...]
     src = slot >> 3
     a = (tile & 3) - (src & 3) & 3
-    b = (tile >> 2 & 3) - (src >> 2 & 3) - a & 3
+    b = (tile >> 2 & 3) - (src >> 2 & 3) + a & 3
     c = (tile >> 4) - (src >> 4) - a & 3
     place = (a | b << 2 | c << 4) * CAP + (slot & 7)
     table = jnp.concatenate([place.astype(F32), weights[...], jnp.zeros((NB - 8, NB), F32)], axis=0).T
@@ -257,25 +260,27 @@
     basis_load.wait()
     lane = lax.broadcasted_iota(jnp.int32, (SEG, 128), 1)
     sub = lax.broadcasted_iota(jnp.int32, (SEG, 128), 0)
-    rows_of = {}
-    third = len(PAIRS) // 3
-    for part in range(3):
-        pairs = PAIRS[part * third : (part + 1) * third]
-
-        def gram_step(n, acc, pairs=pairs):
-            level = n >> 3
-            at = pl.multiple_of((n & 7) * 128, 128)
-            used = sorted({i for p in pairs for i in p[1:]})
-            vals = {i: basis_v[i, level, :, pl.ds(at, 128)].astype(F32) for i in used}
-            out = []
-            for (_, i, j), a in zip(pairs, acc):
-                p = vals[i] * vals[j]
-                out.append(a + (p[:8] + p[8:]))
-            return tuple(out)
-
-        acc = lax.fori_loop(0, 64, gram_step, tuple(jnp.zeros((8, 128), F32) for _ in pairs))
-        for (k, i, _), a in zip(pairs, acc):
-            rows_of[k, i] = jnp.sum(a, axis=0, keepdims=True)
+
+    def gram_step(n, acc):
+        level = n >> 2
+        at = pl.multiple_of((n & 3) * 256, 256)
+        x = jnp.concatenate([basis_v[i, level, :, pl.ds(at, 256)] for i in range(VECS)], axis=0)
+        gram_v[...] += lax.dot_general(x, x, (((1,), (1,)), ((), ())), preferred_element_type=F32)
+        return acc
+
+    span = VECS * ROWS
+    gram_v[...] = jnp.zeros((span, span), F32)
+    lax.fori_loop(0, 32, gram_step, 0)
+    row_of = lax.broadcasted_iota(jnp.int32, (ROWS, span), 0)
+    col_of = lax.broadcasted_iota(jnp.int32, (ROWS, span), 1)
+    diagonal = row_of == (col_of & ROWS - 1)
+    picked = [
+        jnp.sum(jnp.where(diagonal, gram_v[i * ROWS : (i + 1) * ROWS, :], 0.0), axis=0, keepdims=True)
+        for i in range(VECS)
+    ]
+    picked = jnp.concatenate(picked + [jnp.zeros((SEG - VECS, span), F32)], axis=0)
+    gather = lax.broadcasted_iota(jnp.int32, (span, 128), 0) >> 4 == lax.broadcasted_iota(jnp.int32, (span, 128), 1)
+    square = jnp.dot(picked, gather.astype(F32), precision=lax.Precision.HIGHEST, preferred_element_type=F32)
     empty = jnp.zeros((1, 128), F32)
 
     def to_lanes(rows_, k):
@@ -284,7 +289,16 @@
 
     gram = jnp.zeros((SEG, 128), F32)
     for k in range(VECS // 2 + 1):
-        gram = gram + to_lanes([rows_of[k, i] for i in range(VECS) if (k, i) in rows_of], k)
+        other = jnp.where(sub + k >= VECS, sub + k - VECS, sub + k)
+        own = sub < (VECS if k < VECS // 2 else VECS // 2)
+        col = jnp.sum(jnp.where((lane == other) & own, square, 0.0), axis=1, keepdims=True)
+        gram = gram + jnp.where(lane == sub + SEG * k, col, 0.0)
+
+    for c in swap:
+        c.wait()
+    clear_ends(deep)
+    for l in range(FLUX, LEV):
+        x2[l] = maskf[...] * (stencil(x1, l, kap[...]) + mixed(x1, vmix, l, LEV))
 
     def edge_step(i, carry):
         for l in range(FLUX):
@@ -315,10 +329,10 @@
     border = jnp.concatenate([sums[:8], sums[-8:]], axis=0) + times(ends_high, ends_low, *tail)
     for end in (0, 1):
         for i in range(FLUX):
-            edge_out[end, i] = edge_m[end] * border[end * 8 : end * 8 + 8, i * 128 : (i + 1) * 128]
+            edge_out[end, i] = edge_x[end, i] + edge_m[end] * border[end * 8 : end * 8 + 8, i * 128 : (i + 1) * 128]
     edges = [
-        remote(edge_out.at[0], edge_in.at[1], halo.at[12], halo.at[13], comp, above),
-        remote(edge_out.at[1], edge_in.at[0], halo.at[14], halo.at[15], comp, below),
+        remote(edge_out.at[0], edge_in.at[1], halo.at[2, 0], halo.at[2, 1], comp, above),
+        remote(edge_out.at[1], edge_in.at[0], halo.at[2, 2], halo.at[2, 3], comp, below),
     ]
     for c in edges:
         c.start()
@@ -332,9 +346,9 @@
             f[i, :, cut] = piece
             fh[i, 8:24, cut] = maskf[:, cut] * piece
     for l in range(LEV):
-        z = mixed(fh, vmix, l, FLUX, 8, ROWS)
+        z = mixed(fh, vmix, l, FLUX)
         if l < FLUX:
-            z = z + stencil(fh, l, kap[...], 8, ROWS) + f[l]
+            z = z + stencil(fh, l, kap[...]) + f[l]
         x2[l] = x2[l] + maskf[...] * z
 
     def dot_step(n, acc):
@@ -397,20 +411,25 @@
     wait_bytes(bucket, send)
 
 
-def finish(x2, basis_v, result, direction, coefs, out, store):
-    coefs[...] = result[SEG, :VECS]
+def finish(x2, basis_v, result, direction, coefs, out, line, store, small):
+    line[...] = result[SEG, :VECS]
+    first = pltpu.make_async_copy(line, coefs, small)
+    first.start()
+    weigh = [jnp.broadcast_to(result[i : i + 1], (ROWS, 128)) for i in range(VECS + 1)]
     for l in range(LEV):
 
         def part(n, carry):
-            at = pl.multiple_of(n * 128, 128)
-            w = result[VECS : VECS + 1] * x2[l, :, pl.ds(at, 128)]
-            for i in range(VECS):
-                w = w - result[i : i + 1] * basis_v[i, l, :, pl.ds(at, 128)].astype(F32)
-            out[l, :, pl.ds(at, 128)] = w
+            for half in (0, 1):
+                at = pl.multiple_of(n * 256 + half * 128, 128)
+                w = weigh[VECS] * x2[l, :, pl.ds(at, 128)]
+                for i in range(VECS):
+                    w = w - weigh[i] * basis_v[i, l, :, pl.ds(at, 128)].astype(F32)
+                out[l, :, pl.ds(at, 128)] = w
             return carry
 
-        lax.fori_loop(0, 8, part, 0)
+        lax.fori_loop(0, 4, part, 0)
         pltpu.make_async_copy(out.at[l], direction.at[0, l], store).start()
+    first.wait()
     wait_bytes(out, store)
 
 
@@ -422,7 +441,7 @@
     ints = jnp.int32
     scratch = [((4, NB), ints), ((4, NB), F32), None, None, (pad, F32), (pad, F32)]
     scratch += [((FLUX, 32, COLS), F32), ((FLUX, ROWS, COLS), F32), (band, F32), (band, ints), (band, F32)]
-    scratch += [((2, 1, COLS), F32), ((2, 1, COLS), ints), ((8, FLUX, ROWS, 128), F32)]
+    scratch += [((VECS * ROWS, VECS * ROWS), F32), ((2, FLUX, 8, 128), F32), ((8, FLUX, ROWS, 128), F32)]
     scratch += [((TILES, FLUX, CAP, 128), F32)] * 2 + [((FLUX * NB, 128), F32)]
     scratch += [((VECS, FLUX, 2, 8, 128), F32)] + [((2, FLUX, 8, 128), F32)] * 2 + [((2, 8, 128), F32)] * 2
     scratch += [((FLUX, 2, 8, 128), F32)]
@@ -439,7 +458,7 @@
         ),
         in_specs=[pl.BlockSpec(memory_space=pltpu.HBM)] * 8,
         out_specs=(vmem,) * 3,
-        scratch_shapes=scratch + [dma((9,)), dma(()), dma((GROUPS,)), dma((16,)), dma((6,))],
+        scratch_shapes=scratch + [dma((9,)), dma(()), dma((GROUPS,)), dma((3, 4)), dma((6,))],
         compiler_params=pltpu.CompilerParams(
             collective_id=0, has_side_effects=True, vmem_limit_bytes=24 << 20
         ),
@@ -466,8 +485,8 @@
             jax.ShapeDtypeStruct((VECS,), F32),
         ),
         in_specs=[vmem] * 3,
-        out_specs=(pl.BlockSpec(memory_space=pl.ANY), vmem),
-        scratch_shapes=[pltpu.VMEM((LEV, ROWS, COLS), F32), dma(())],
+        out_specs=(pl.BlockSpec(memory_space=pl.ANY),) * 2,
+        scratch_shapes=[pltpu.VMEM((LEV, ROWS, COLS), F32), pltpu.VMEM((VECS,), F32), dma(()), dma(())],
         compiler_params=pltpu.CompilerParams(vmem_limit_bytes=16 << 20),
         name="finish",
     )(x2, basis_v, result)

time: 43.8 us -> 42.7 us (0.975)
  Pallas kernels: 43.1 us -> 41.9 us
    pallas_call x1, Pallas kernels: 2.52 us -> 1.78 us  [body(): pl.pallas_call(finish, out_shape=(jax.ShapeDtypeStruct((1, LEV, ROWS, COL...]
where the time goes in v4:
time: 42.7 us; the launch traced here: 42.6 us
  Pallas kernels  41.9 us (98%)
  between operations  0.64 us (1%)
    pallas_call x1, Pallas kernels, body(): pl.pallas_call(kernel, out_shape=(jax.ShapeDtypeStruct((LEV, ROWS, COLS),...  40.2 us
    pallas_call x1, Pallas kernels, body(): pl.pallas_call(finish, out_shape=(jax.ShapeDtypeStruct((1, LEV, ROWS, COL...  1.78 us

profile of v4, /device:TPU:1, one launch (start us, length us, event | category | flops | bytes accessed | tf_op | source)
XLA Modules:
  0.0 42.6 jit_solution(11505034783028223419)
XLA Ops:
  0.6 40.2 %interval.1 = (f32[8,16,1024]{2,1,0:T(8,128)S(1)}, bf16[12,8,16,1024]{3,2,1,0:T(8,128)(2,1)S(1)}, f32[24,128]{1,0:T(8,128)S(1)}) custom-call(f32[1,8,16,1024]{3,2,1,0:T(8,128)} %state.1, bf16[12,1,8,16,1024]{4,3,2,1,0:T(8,128)(2,1)} %basis.1, f32[1,16,1024]{2,1,0:T(8,128)} %kappa.1, s32[16,1024]{1,0:T(8,128)} %land.1, s32[1,1,4,128]{3,2,1,0:T(4,128)} %bitcast.4, ...), custom_call_target="tpu_custom_call" | custom-call | tf_op jit(solution)/shard_map/interval/pallas_call | solution.py:452
  40.8 1.8 %finish.1 = (f32[1,8,16,1024]{3,2,1,0:T(8,128)}, f32[12]{0:T(128)}) custom-call(f32[8,16,1024]{2,1,0:T(8,128)S(1)} %get-tuple-element.5.x2, bf16[12,8,16,1024]{3,2,1,0:T(8,128)(2,1)S(1)} %get-tuple-element.6.basis_v, f32[24,128]{1,0:T(8,128)S(1)} %get-tuple-element.7.result), custom_call_target="tpu_custom_call" | custom-call | tf_op jit(solution)/shard_map/finish/pallas_call | solution.py:481

commit v5 on v4

--- a/solution.py
+++ b/solution.py
@@ -30,7 +30,8 @@
 FAR_FIRST = sorted(range(TILES), key=lambda k: -hops(k))
 
 
-PEERS = [sorted((k for k in range(1, TILES) if k & 1 == c), key=lambda k: -hops(k)) for c in (0, 1)]
+FAR = [k for k in FAR_FIRST if hops(k) >= 5]
+NEAR = [k for k in FAR_FIRST if 0 < hops(k) < 5]
 
 
 def offset_of(step):
@@ -53,47 +54,36 @@
     pltpu.make_async_copy(ref, ref, sem).wait()
 
 
-def sum_over_devices(comp, tile, mine, pair, wide, part, other, sems, meanwhile):
+def sum_over_devices(comp, tile, mine, pair, chip, far, near, sems, meanwhile):
     first = remote(mine, pair, sems.at[0], sems.at[1], 1 - comp, tile)
     first.start()
+    for i, k in enumerate(FAR):
+        for c in (0, 1):
+            remote(mine, far.at[pl.ds(2 * i + comp, 1)], sems.at[2], sems.at[3], c, tile ^ k).start()
     first.wait()
-    chip = mine[...] + pair[...]
-    part[...] = chip
-    odd = tile & 1
-    slot = tile >> 1
-
-    for c in (0, 1):
-
-        @pl.when(comp == c)
+    chip[...] = mine[...] + pair[...]
+    own = pl.ds(tile, 1)
+    for core in (0, 1):
+
+        @pl.when(comp == core)
         def _():
-            for k in PEERS[c]:
-                remote(part, wide.at[slot], sems.at[2], sems.at[3], odd, tile ^ k).start()
-
+            for k in NEAR[core::2]:
+                for c in (0, 1):
+                    remote(chip, near.at[own], sems.at[4], sems.at[5], c, tile ^ k).start()
+
+    near[own] = chip[...]
     meanwhile()
-
-    @pl.when(comp == odd)
-    def _():
-        wide[slot] = chip
-        wait_bytes(wide.at[pl.ds(0, TILES // 2 - 1)], sems.at[3])
-
-    @pl.when(comp != odd)
-    def _():
-        wait_bytes(wide.at[pl.ds(0, TILES // 2)], sems.at[3])
-
-    half = wide[0]
-    for s in range(1, TILES // 2):
-        half = half + wide[s]
-    for c in (0, 1):
-
-        @pl.when(comp == c)
-        def _():
-            wait_bytes(wide.at[pl.ds(0, len(PEERS[c]))], sems.at[2])
-
-    part[...] = half
-    last = remote(part, other, sems.at[4], sems.at[5], 1 - comp, tile)
-    last.start()
-    last.wait()
-    return half + other[...]
+    wait_bytes(far.at[pl.ds(0, 2 * len(FAR))], sems.at[3])
+    for i, k in enumerate(FAR):
+        near[pl.ds(tile ^ k, 1)] = far[2 * i : 2 * i + 1] + far[2 * i + 1 : 2 * i + 2]
+    wait_bytes(near.at[pl.ds(0, len(NEAR))], sems.at[5])
+    total = jnp.sum(near[...], axis=0, keepdims=True)
+    return total
+
+
+def wait_sums(far, near, sems):
+    wait_bytes(far.at[pl.ds(0, 2 * len(FAR))], sems.at[2])
+    wait_bytes(near.at[pl.ds(0, len(NEAR))], sems.at[4])
 
 
 def stencil(ref, level, kap):
@@ -120,7 +110,7 @@
     x2, basis_v, result,
     slots, weights, vmix, rows, x0, x1, fh, f, kap, land_v, maskf, gram_v, edge_x,
     surf, bucket, arrived, imp, edge_b, edge_out, edge_in, edge_k, edge_m, near,
-    e_mine, e_pair, e_wide, e_part, e_other,
+    e_mine, e_pair, e_chip, e_far, e_near,
     load, send, recv, halo, esem,
 ):
     comp = lax.axis_index("comp")
@@ -170,14 +160,28 @@
         c.wait()
     pl.semaphore_wait(barrier, TILES + 2)
 
+    def when_above(f):
+        pl.when(tile > 0)(f)
+
+    def when_below(f):
+        pl.when(tile < TILES - 1)(f)
+
+    def start_pair(up, down):
+        when_above(up.start)
+        when_below(down.start)
+        return up, down
+
+    def wait_pair(up, down):
+        when_below(up.wait_recv)
+        when_above(down.wait_recv)
+        when_above(up.wait_send)
+        when_below(down.wait_send)
+
     def swap_rows(ref, sems):
-        pair = [
+        return start_pair(
             remote(ref.at[:, pl.ds(8, 1), :], ref.at[:, pl.ds(24, 1), :], sems.at[0], sems.at[1], comp, above),
             remote(ref.at[:, pl.ds(23, 1), :], ref.at[:, pl.ds(7, 1), :], sems.at[2], sems.at[3], comp, below),
-        ]
-        for c in pair:
-            c.start()
-        return pair
+        )
 
     def clear_ends(ref):
         n = ref.shape[0]
@@ -212,8 +216,7 @@
     kap_load.wait()
     land_load.wait()
     maskf[...] = jnp.where(comp == 0, land_v[...].astype(F32), jnp.ones((ROWS, COLS), F32))
-    for c in swap:
-        c.wait()
+    wait_pair(*swap)
     clear_ends(x0)
     for l in range(LEV):
         x1[l, 8:24, :] = maskf[...] * (stencil(x0, l, kap[...]) + mixed(x0, vmix, l, LEV))
@@ -294,8 +297,7 @@
         col = jnp.sum(jnp.where((lane == other) & own, square, 0.0), axis=1, keepdims=True)
         gram = gram + jnp.where(lane == sub + SEG * k, col, 0.0)
 
-    for c in swap:
-        c.wait()
+    wait_pair(*swap)
     clear_ends(deep)
     for l in range(FLUX, LEV):
         x2[l] = maskf[...] * (stencil(x1, l, kap[...]) + mixed(x1, vmix, l, LEV))
@@ -330,12 +332,10 @@
     for end in (0, 1):
         for i in range(FLUX):
             edge_out[end, i] = edge_x[end, i] + edge_m[end] * border[end * 8 : end * 8 + 8, i * 128 : (i + 1) * 128]
-    edges = [
+    edges = start_pair(
         remote(edge_out.at[0], edge_in.at[1], halo.at[2, 0], halo.at[2, 1], comp, above),
         remote(edge_out.at[1], edge_in.at[0], halo.at[2, 2], halo.at[2, 3], comp, below),
-    ]
-    for c in edges:
-        c.start()
+    )
     sums = sums + times(high, low, *tail)
     for i in range(FLUX):
         imp[i * NB : (i + 1) * NB, :] = sums[:, i * 128 : (i + 1) * 128]
@@ -366,13 +366,11 @@
         for end, row in ((0, 0), (1, 15)):
             for j in every:
                 near[l, end, j : j + 1] = x2[l, row : row + 1, j * 128 : (j + 1) * 128]
-    for c in edges:
-        c.wait()
+    wait_pair(*edges)
     extra = {}
     for end, last in ((0, 0), (1, TILES - 1)):
-        factor = jnp.where(tile == last, jnp.zeros((8, 128), F32), edge_k[end])
         for l in range(FLUX):
-            add = factor * edge_in[end, l]
+            add = jnp.where(tile == last, jnp.zeros((8, 128), F32), edge_k[end] * edge_in[end, l])
             extra[l, end] = add
             for i in range(VECS):
                 acc[i] = acc[i] + edge_b[i, l, end] * add
@@ -387,7 +385,7 @@
             for j in every:
                 x2[l, row : row + 1, j * 128 : (j + 1) * 128] = full[j : j + 1]
 
-    dots = sum_over_devices(comp, tile, e_mine, e_pair, e_wide, e_part, e_other, esem, add_edges)
+    dots = sum_over_devices(comp, tile, e_mine, e_pair, e_chip, e_far, e_near, esem, add_edges)
 
     one = lax.broadcasted_iota(jnp.int32, (1, 128), 1)
     seg, pos = one >> 4, one & 15
@@ -408,6 +406,7 @@
     column = jnp.sum(jnp.where(lane == sub, jnp.broadcast_to(line, (SEG, 128)), 0.0), axis=1, keepdims=True)
     result[0:SEG] = jnp.broadcast_to(column * scale, (SEG, 128))
     result[SEG : SEG + 1] = coef
+    wait_sums(e_far, e_near, esem)
     wait_bytes(bucket, send)
 
 
@@ -445,7 +444,7 @@
     scratch += [((TILES, FLUX, CAP, 128), F32)] * 2 + [((FLUX * NB, 128), F32)]
     scratch += [((VECS, FLUX, 2, 8, 128), F32)] + [((2, FLUX, 8, 128), F32)] * 2 + [((2, 8, 128), F32)] * 2
     scratch += [((FLUX, 2, 8, 128), F32)]
-    scratch += [((1, 128), F32)] * 2 + [((TILES // 2, 1, 128), F32)] + [((1, 128), F32)] * 2
+    scratch += [((1, 128), F32)] * 3 + [((16, 128), F32), ((TILES, 128), F32)]
     scratch = [pltpu.VMEM(*v) if v else None for v in scratch]
     scratch[2] = pltpu.SMEM((LEV, LEV), F32)
     scratch[3] = pltpu.SMEM((CAP, TILES), ints)

time: 42.7 us -> 41.1 us (0.963)
  Pallas kernels: 41.9 us -> 40.4 us
    pallas_call x1, Pallas kernels: 40.2 us -> 38.6 us  [body(): pl.pallas_call(kernel, out_shape=(jax.ShapeDtypeStruct((LEV, ROWS, COLS),...]
where the time goes in v5:
time: 41.1 us; the launch traced here: 41 us
  Pallas kernels  40.4 us (98%)
  between operations  0.64 us (2%)
    pallas_call x1, Pallas kernels, body(): pl.pallas_call(kernel, out_shape=(jax.ShapeDtypeStruct((LEV, ROWS, COLS),...  38.6 us
    pallas_call x1, Pallas kernels, body(): pl.pallas_call(finish, out_shape=(jax.ShapeDtypeStruct((1, LEV, ROWS, COL...  1.78 us

profile of v5, /device:TPU:1, one launch (start us, length us, event | category | flops | bytes accessed | tf_op | source)
XLA Modules:
  0.0 41.0 jit_solution(16334082873720052013)
XLA Ops:
  0.6 38.6 %interval.1 = (f32[8,16,1024]{2,1,0:T(8,128)S(1)}, bf16[12,8,16,1024]{3,2,1,0:T(8,128)(2,1)S(1)}, f32[24,128]{1,0:T(8,128)S(1)}) custom-call(f32[1,8,16,1024]{3,2,1,0:T(8,128)} %state.1, bf16[12,1,8,16,1024]{4,3,2,1,0:T(8,128)(2,1)} %basis.1, f32[1,16,1024]{2,1,0:T(8,128)} %kappa.1, s32[16,1024]{1,0:T(8,128)} %land.1, s32[1,1,4,128]{3,2,1,0:T(4,128)} %bitcast.4, ...), custom_call_target="tpu_custom_call" | custom-call | tf_op jit(solution)/shard_map/interval/pallas_call | solution.py:451
  39.2 1.8 %finish.1 = (f32[1,8,16,1024]{3,2,1,0:T(8,128)}, f32[12]{0:T(128)}) custom-call(f32[8,16,1024]{2,1,0:T(8,128)S(1)} %get-tuple-element.5.x2, bf16[12,8,16,1024]{3,2,1,0:T(8,128)(2,1)S(1)} %get-tuple-element.6.basis_v, f32[24,128]{1,0:T(8,128)S(1)} %get-tuple-element.7.result), custom_call_target="tpu_custom_call" | custom-call | tf_op jit(solution)/shard_map/finish/pallas_call | solution.py:480

commit v6 on v5

--- a/solution.py
+++ b/solution.py
@@ -17,6 +17,7 @@
 NB = 128
 GROUPS = 4
 PER = TILES // GROUPS
+EARLY = 48
 MESH = pl.DeviceIdType.MESH
 F32 = jnp.float32
 BF16 = jnp.bfloat16
@@ -107,9 +108,9 @@
 
 def kernel(
     state, basis, kappa, land, slots_hbm, weights_hbm, vmix_hbm, rows_hbm,
-    x2, basis_v, result,
+    x2, wide, result,
     slots, weights, vmix, rows, x0, x1, fh, f, kap, land_v, maskf, gram_v, edge_x,
-    surf, bucket, arrived, imp, edge_b, edge_out, edge_in, edge_k, edge_m, near,
+    basis_v, surf, bucket, arrived, imp, edge_b, edge_out, edge_in, edge_k, edge_m, near,
     e_mine, e_pair, e_chip, e_far, e_near,
     load, send, recv, halo, esem,
 ):
@@ -126,7 +127,6 @@
         for k in ks:
             pl.semaphore_signal(barrier, inc=1, device_id=(1 - comp, tile ^ k), device_id_type=MESH)
 
-    greet(FAR_FIRST[:32])
     surf_loads = [
         pltpu.make_async_copy(
             state.at[0, pl.ds(0, FLUX), :, pl.ds(128 * j, 128)], surf.at[j], load.at[0]
@@ -135,11 +135,12 @@
     ]
     rows_load = pltpu.make_async_copy(rows_hbm.at[0, 0], rows, load.at[5])
     x_load = pltpu.make_async_copy(state.at[0], x0.at[:, pl.ds(8, ROWS), :], load.at[1])
-    for c in [rows_load, x_load, *surf_loads]:
+    greet(FAR_FIRST)
+    for c in [rows_load, *surf_loads]:
         c.start()
-    greet(FAR_FIRST[32:])
     for t in (above, below):
         pl.semaphore_signal(barrier, inc=1, device_id=(comp, t), device_id_type=MESH)
+    x_load.start()
     kap_load = pltpu.make_async_copy(kappa.at[0], kap, load.at[2])
     kap_load.start()
     land_load = pltpu.make_async_copy(land, land_v, load.at[3])
@@ -153,7 +154,6 @@
     for c in table_loads:
         c.start()
     basis_load = pltpu.make_async_copy(basis.at[:, 0], basis_v, load.at[4])
-    basis_load.start()
     rows_load.wait()
     x_load.wait()
     for c in surf_loads:
@@ -210,7 +210,8 @@
         remote(bucket.at[step], arrived.at[step], send, recv.at[step >> 4], 1 - comp, dest).start()
         return carry
 
-    lax.fori_loop(0, TILES // 2, deliver, 0)
+    basis_load.start()
+    lax.fori_loop(0, EARLY, deliver, 0)
 
     vmix_load.wait()
     kap_load.wait()
@@ -225,7 +226,7 @@
         x1[0:FLUX, row : row + 1, :] = jnp.zeros((FLUX, 1, COLS), F32)
         fh[:, row : row + 1, :] = jnp.zeros((FLUX, 1, COLS), F32)
     swap = swap_rows(deep, halo.at[1])
-    lax.fori_loop(TILES // 2, TILES, deliver, 0)
+    lax.fori_loop(EARLY, TILES, deliver, 0)
 
     for j in every:
         cut = slice(j * 128, (j + 1) * 128)
@@ -378,7 +379,13 @@
     sums_of = [jnp.sum(a, axis=0, keepdims=True) for a in acc]
     e_mine[...] = jnp.sum(gram + to_lanes(sums_of, 7), axis=0, keepdims=True)
 
+    def widen(i, carry):
+        for l in range(LEV):
+            wide[i, l] = basis_v[i, l].astype(F32)
+        return carry
+
     def add_edges():
+        lax.fori_loop(0, VECS, widen, 0)
         for (l, end), add in extra.items():
             row = 15 * end
             full = near[l, end] + add
@@ -410,7 +417,7 @@
     wait_bytes(bucket, send)
 
 
-def finish(x2, basis_v, result, direction, coefs, out, line, store, small):
+def finish(x2, wide, result, direction, coefs, out, line, store, small):
     line[...] = result[SEG, :VECS]
     first = pltpu.make_async_copy(line, coefs, small)
     first.start()
@@ -422,7 +429,7 @@
                 at = pl.multiple_of(n * 256 + half * 128, 128)
                 w = weigh[VECS] * x2[l, :, pl.ds(at, 128)]
                 for i in range(VECS):
-                    w = w - weigh[i] * basis_v[i, l, :, pl.ds(at, 128)].astype(F32)
+                    w = w - weigh[i] * wide[i, l, :, pl.ds(at, 128)]
                 out[l, :, pl.ds(at, 128)] = w
             return carry
 
@@ -440,7 +447,8 @@
     ints = jnp.int32
     scratch = [((4, NB), ints), ((4, NB), F32), None, None, (pad, F32), (pad, F32)]
     scratch += [((FLUX, 32, COLS), F32), ((FLUX, ROWS, COLS), F32), (band, F32), (band, ints), (band, F32)]
-    scratch += [((VECS * ROWS, VECS * ROWS), F32), ((2, FLUX, 8, 128), F32), ((8, FLUX, ROWS, 128), F32)]
+    scratch += [((VECS * ROWS, VECS * ROWS), F32), ((2, FLUX, 8, 128), F32)]
+    scratch += [((VECS, LEV, ROWS, COLS), BF16), ((8, FLUX, ROWS, 128), F32)]
     scratch += [((TILES, FLUX, CAP, 128), F32)] * 2 + [((FLUX * NB, 128), F32)]
     scratch += [((VECS, FLUX, 2, 8, 128), F32)] + [((2, FLUX, 8, 128), F32)] * 2 + [((2, 8, 128), F32)] * 2
     scratch += [((FLUX, 2, 8, 128), F32)]
@@ -448,11 +456,11 @@
     scratch = [pltpu.VMEM(*v) if v else None for v in scratch]
     scratch[2] = pltpu.SMEM((LEV, LEV), F32)
     scratch[3] = pltpu.SMEM((CAP, TILES), ints)
-    x2, basis_v, result = pl.pallas_call(
+    x2, wide, result = pl.pallas_call(
         kernel,
         out_shape=(
             jax.ShapeDtypeStruct((LEV, ROWS, COLS), F32),
-            jax.ShapeDtypeStruct((VECS, LEV, ROWS, COLS), BF16),
+            jax.ShapeDtypeStruct((VECS, LEV, ROWS, COLS), F32),
             jax.ShapeDtypeStruct((SEG + 8, 128), F32),
         ),
         in_specs=[pl.BlockSpec(memory_space=pltpu.HBM)] * 8,
@@ -488,7 +496,7 @@
         scratch_shapes=[pltpu.VMEM((LEV, ROWS, COLS), F32), pltpu.VMEM((VECS,), F32), dma(()), dma(())],
         compiler_params=pltpu.CompilerParams(vmem_limit_bytes=16 << 20),
         name="finish",
-    )(x2, basis_v, result)
+    )(x2, wide, result)
 
 
 def solution(mesh):

time: 41.1 us -> 40.6 us (0.988)
  Pallas kernels: 40.4 us -> 39.8 us
    pallas_call x1, Pallas kernels: 38.6 us -> 38.1 us  [body(): pl.pallas_call(kernel, out_shape=(jax.ShapeDtypeStruct((LEV, ROWS, COLS),...]
where the time goes in v6:
time: 40.6 us; the launch traced here: 40.5 us
  Pallas kernels  39.8 us (98%)
  between operations  0.64 us (2%)
    pallas_call x1, Pallas kernels, body(): pl.pallas_call(kernel, out_shape=(jax.ShapeDtypeStruct((LEV, ROWS, COLS),...  38.1 us
    pallas_call x1, Pallas kernels, body(): pl.pallas_call(finish, out_shape=(jax.ShapeDtypeStruct((1, LEV, ROWS, COL...  1.72 us

profile of v6, /device:TPU:1, one launch (start us, length us, event | category | flops | bytes accessed | tf_op | source)
XLA Modules:
  0.0 40.5 jit_solution(5123456440928983978)
XLA Ops:
  0.6 38.1 %interval.1 = (f32[8,16,1024]{2,1,0:T(8,128)S(1)}, f32[12,8,16,1024]{3,2,1,0:T(8,128)S(1)}, f32[24,128]{1,0:T(8,128)S(1)}) custom-call(f32[1,8,16,1024]{3,2,1,0:T(8,128)} %state.1, bf16[12,1,8,16,1024]{4,3,2,1,0:T(8,128)(2,1)} %basis.1, f32[1,16,1024]{2,1,0:T(8,128)} %kappa.1, s32[16,1024]{1,0:T(8,128)} %land.1, s32[1,1,4,128]{3,2,1,0:T(4,128)} %bitcast.4, ...), custom_call_target="tpu_custom_call" | custom-call | tf_op jit(solution)/shard_map/interval/pallas_call | solution.py:459
  38.7 1.7 %finish.1 = (f32[1,8,16,1024]{3,2,1,0:T(8,128)}, f32[12]{0:T(128)}) custom-call(f32[8,16,1024]{2,1,0:T(8,128)S(1)} %get-tuple-element.5.x2, f32[12,8,16,1024]{3,2,1,0:T(8,128)S(1)} %get-tuple-element.6.wide, f32[24,128]{1,0:T(8,128)S(1)} %get-tuple-element.7.result), custom_call_target="tpu_custom_call" | custom-call | tf_op jit(solution)/shard_map/finish/pallas_call | solution.py:488

commit v7 on v6

--- a/solution.py
+++ b/solution.py
@@ -136,10 +136,10 @@
     rows_load = pltpu.make_async_copy(rows_hbm.at[0, 0], rows, load.at[5])
     x_load = pltpu.make_async_copy(state.at[0], x0.at[:, pl.ds(8, ROWS), :], load.at[1])
     greet(FAR_FIRST)
+    for t in (above, below):
+        pl.semaphore_signal(barrier, inc=1, device_id=(comp, t), device_id_type=MESH)
     for c in [rows_load, *surf_loads]:
         c.start()
-    for t in (above, below):
-        pl.semaphore_signal(barrier, inc=1, device_id=(comp, t), device_id_type=MESH)
     x_load.start()
     kap_load = pltpu.make_async_copy(kappa.at[0], kap, load.at[2])
     kap_load.start()
@@ -426,14 +426,15 @@
 
         def part(n, carry):
             for half in (0, 1):
-                at = pl.multiple_of(n * 256 + half * 128, 128)
+                at = n * 256 + half * 128
                 w = weigh[VECS] * x2[l, :, pl.ds(at, 128)]
                 for i in range(VECS):
                     w = w - weigh[i] * wide[i, l, :, pl.ds(at, 128)]
                 out[l, :, pl.ds(at, 128)] = w
             return carry
 
-        lax.fori_loop(0, 4, part, 0)
+        for n in range(4):
+            part(n, 0)
         pltpu.make_async_copy(out.at[l], direction.at[0, l], store).start()
     first.wait()
     wait_bytes(out, store)

time: 40.6 us -> 40 us (0.985)
  Pallas kernels: 39.8 us -> 39.2 us
    pallas_call x1, Pallas kernels: 1.72 us -> 1.08 us  [body(): pl.pallas_call(finish, out_shape=(jax.ShapeDtypeStruct((1, LEV, ROWS, COL...]
where the time goes in v7:
time: 40 us; the launch traced here: 39.8 us
  Pallas kernels  39.2 us (98%)
  between operations  0.64 us (2%)
    pallas_call x1, Pallas kernels, body(): pl.pallas_call(kernel, out_shape=(jax.ShapeDtypeStruct((LEV, ROWS, COLS),...  38.1 us
    pallas_call x1, Pallas kernels, body(): pl.pallas_call(finish, out_shape=(jax.ShapeDtypeStruct((1, LEV, ROWS, COL...  1.08 us

profile of v7, /device:TPU:1, one launch (start us, length us, event | category | flops | bytes accessed | tf_op | source)
XLA Modules:
  0.0 39.8 jit_solution(10732651698544782553)
XLA Ops:
  0.6 38.1 %interval.1 = (f32[8,16,1024]{2,1,0:T(8,128)S(1)}, f32[12,8,16,1024]{3,2,1,0:T(8,128)S(1)}, f32[24,128]{1,0:T(8,128)S(1)}) custom-call(f32[1,8,16,1024]{3,2,1,0:T(8,128)} %state.1, bf16[12,1,8,16,1024]{4,3,2,1,0:T(8,128)(2,1)} %basis.1, f32[1,16,1024]{2,1,0:T(8,128)} %kappa.1, s32[16,1024]{1,0:T(8,128)} %land.1, s32[1,1,4,128]{3,2,1,0:T(4,128)} %bitcast.4, ...), custom_call_target="tpu_custom_call" | custom-call | tf_op jit(solution)/shard_map/interval/pallas_call | solution.py:460
  38.8 1.1 %finish.1 = (f32[1,8,16,1024]{3,2,1,0:T(8,128)}, f32[12]{0:T(128)}) custom-call(f32[8,16,1024]{2,1,0:T(8,128)S(1)} %get-tuple-element.5.x2, f32[12,8,16,1024]{3,2,1,0:T(8,128)S(1)} %get-tuple-element.6.wide, f32[24,128]{1,0:T(8,128)S(1)} %get-tuple-element.7.result), custom_call_target="tpu_custom_call" | custom-call | tf_op jit(solution)/shard_map/finish/pallas_call | solution.py:489
